TPU v7x, 32 devices: a whole 2x2x4 slice. The times are simulated.
32 devices in a mesh: dom: 8 (over z, x), feat: 4 (over y, core).
Axes of the slice: x: 2, y: 2, z: 4, core: 2. Of those that a mesh axis runs over, the one named last changes fastest.
Arguments:
- features: bfloat16 [8192, 1024], P('dom', 'feat'), may hold values from -6 to 6
- adjacency: bfloat16 [64, 16, 128, 128], P('dom'), may hold values from -0.125 to 0.125
- tile_src: int32 [64, 16], replicated, may hold values from 0 to 63, as said below
- mig_slot: int32 [8, 2], replicated, may hold values from 0 to 7, as said below
- weight_one: bfloat16 [1024, 1024], replicated, may hold values from -0.1875 to 0.1875
- weight_two: bfloat16 [1024, 1024], replicated, may hold values from -0.1875 to 0.1875
Outputs:
- mixed: bfloat16 [8192, 1024], P('dom', 'feat')
Inputs may be any that keep to these rules, and one draw needn't show every extreme that they name: `tile_src`: the tiles of the row blocks that one partition holds name at most 2 distinct blocks held by any one other partition, both in the starting placement and in the placement after the move; in the starting placement they name exactly 2 blocks of every other partition, one of which leaves that partition in the move. `mig_slot`: each row holds 2 distinct slots.
All inputs are finite; a program needn't handle non-finite values.
Results may differ from a plain program's by a relative error of at most 0.0064.
Values may be sent and summed in bfloat16 or wider, within the bound.
No kernel may reach another device: no remote copies, remote signals or barrier semaphores. Data moves between devices by JAX's collectives and lax.ppermute only.
A program may use at most 128 MiB of HBM per device.

v0:
```python
import functools

import jax
import jax.numpy as jnp
from jax import lax
from jax.experimental import pallas as pl
from jax.experimental.pallas import tpu as pltpu
from jax.sharding import PartitionSpec as P


BF16 = jnp.bfloat16
F32 = jnp.float32
I32 = jnp.int32
VMEM = pl.BlockSpec(memory_space=pltpu.VMEM)
SMEM = pl.BlockSpec(memory_space=pltpu.SMEM)
ANY = pl.BlockSpec(memory_space=pl.ANY)
HBM = pl.BlockSpec(memory_space=pltpu.HBM)


def swap(value, axis, flip):
    return lax.ppermute(value, axis, [(i, i ^ flip) for i in range(lax.axis_size(axis))])


def block(shape, dtype=BF16):
    return pltpu.VMEM(shape, dtype)


def scalars(shape):
    return pltpu.SMEM(shape, I32)


def copy_all(*triples):
    copies = [pltpu.make_async_copy(*triple) for triple in triples]
    for copy in copies:
        copy.start()
    for copy in copies:
        copy.wait()


def load_kernel(tiles_ref, mig_ref, x_ref, named_ref, slots_ref, own_ref, pair_ref, sems):
    copy_all(
        (tiles_ref, named_ref, sems.at[0]),
        (mig_ref, slots_ref, sems.at[1]),
        (x_ref, own_ref, sems.at[2]),
    )
    me = lax.axis_index("dom")
    for m in range(2):
        pair_ref[m] = own_ref[slots_ref[m, me]]


def write_sends(domains, slots_ref, own_ref, near_refs, far_refs):
    half = domains // 2
    for k in range(1, half):
        near_refs[k - 1][0] = own_ref[slots_ref[2 * k]]
        near_refs[k - 1][1] = own_ref[slots_ref[2 * k + 1]]
    for k in range(half, domains):
        far_refs[k - half][0] = own_ref[slots_ref[2 * k + 1]]


def first_kernel(domains, rows, mig, tiles_ref, own_ref, slots_ref, which_ref, deal_ref, *sends):
    half = domains // 2
    me = lax.axis_index("dom")
    mine0, mine1 = mig[0, me], mig[1, me]
    slots_ref[0] = mine0
    slots_ref[1] = mine1
    deal_ref[0] = mine0
    deal_ref[1] = mine1
    place = jnp.int32(2)
    for s in range(rows):
        deal_ref[place] = s
        place = place + jnp.where((mine0 == s) | (mine1 == s), 0, 1)
    opposite = me ^ half
    opposite_last = opposite * rows + mig[1, opposite]

    named = tiles_ref[...]
    user = lax.broadcasted_iota(I32, named.shape, 1) // rows
    slot = named - me * rows
    leaves = (slot == mine0) | (slot == mine1)
    staying = jnp.where((slot >= 0) & (slot < rows) & jnp.logical_not(leaves), slot, 0)
    last = jnp.where(slot == mine1, 1, 0)
    relayed = jnp.where(named == opposite_last, 1, 0)

    def requests(k):
        asks = user == (me ^ k)
        slots_ref[2 * k + 1] = jnp.max(jnp.where(asks, staying, 0))
        slots_ref[2 * k] = jnp.where(jnp.max(jnp.where(asks, last, 0)) == 1, mine1, mine0)
        which_ref[k] = jnp.max(jnp.where(asks, relayed, 0))

    if domains <= 16:
        for k in range(1, domains):
            requests(k)
    else:
        pl.loop(1, domains)(requests)
    write_sends(domains, slots_ref, own_ref, sends[: half - 1], sends[half - 1 :])


def table_kernel(domains, rows, mig, tiles_ref, *refs):
    sources, table_ref, targets, found_ref, sems = refs[:3], refs[3], refs[4:7], refs[7], refs[8]
    loads = [
        pltpu.make_async_copy(source, target, sems.at[n])
        for n, (source, target) in enumerate(zip(sources, targets))
    ]
    for load in loads:
        load.start()
    half = domains // 2
    named = tiles_ref[...]
    user = lax.broadcasted_iota(I32, named.shape, 1) // rows
    holder = named // rows
    slot = named - holder * rows
    flip = holder ^ user

    def mark(q, carry):
        first, last = carry
        here = holder == q
        first = first | (here & (slot == mig[0, q])).astype(I32)
        last = last | (here & (slot == mig[1, q])).astype(I32)
        return first, last

    zeros = jnp.zeros_like(named)
    first, last = lax.fori_loop(0, domains, mark, (zeros, zeros))
    leaves = first | last
    place = rows + 2 * flip + 1 - leaves
    place = jnp.where((flip == half) & (leaves == 1), rows + last, place)
    found_ref[...] = jnp.where(flip == 0, slot, place)
    copy_all((found_ref, table_ref, sems.at[3]))
    for load in loads:
        load.wait()


def relay_kernel(half, which_ref, pair_ref, *outs):
    for k in range(1, half):
        outs[k - 1][0] = pair_ref[which_ref[k]]


def fill_early_kernel(domains, own_ref, *refs):
    *arrived, pool_ref = refs
    half = domains // 2
    rows = own_ref.shape[0]
    pool_ref[0:rows] = own_ref[...]
    pool_ref[rows : rows + 2] = arrived[0][...]
    for k in range(1, half):
        pool_ref[rows + 2 * k : rows + 2 * k + 2] = arrived[k][...]
    pool_ref[rows + 2 * half + 1] = arrived[half][0]
    for k in range(half + 2, domains):
        pool_ref[rows + 2 * k + 1] = arrived[k - 1][0]


def fill_late(domains, rows, late, pool_ref):
    half = domains // 2
    pool_ref[rows + 2 * (half + 1) + 1] = late[0][0]
    for k in range(1, half):
        pool_ref[rows + 2 * (half + k)] = late[k][0]


def sum_row(r, table_ref, adjacency_ref, pool_ref):
    rows, tiles = adjacency_ref.shape[:2]
    g = lax.axis_index("dom") * rows + r
    total = None
    for t in range(0, tiles, 2):
        left = jnp.concatenate([adjacency_ref[r, t], adjacency_ref[r, t + 1]], axis=1)
        right = jnp.concatenate(
            [pool_ref[table_ref[t, g]], pool_ref[table_ref[t + 1, g]]], axis=0
        )
        part = jnp.dot(left, right, preferred_element_type=F32)
        total = part if total is None else total + part
    return total.astype(BF16)


def first_sum_kernel(domains, feats, part, table_ref, deal_ref, adjacency_ref, *refs):
    _, *late, pool_ref, out_ref = refs
    fill_late(domains, adjacency_ref.shape[0], late, pool_ref)
    part_sum_kernel(feats, [part], table_ref, deal_ref, adjacency_ref, pool_ref, out_ref)


def part_sum_kernel(feats, parts, table_ref, deal_ref, adjacency_ref, pool_ref, *outs):
    for (i, j), out_ref in zip(parts, outs, strict=True):
        row = deal_ref[i * feats + (lax.axis_index("feat") ^ j)]
        out_ref[0] = sum_row(row, table_ref, adjacency_ref, pool_ref)


def leaving_sum_kernel(domains, table_ref, slots_ref, adjacency_ref, *refs):
    _, *late, pool_ref, out_ref = refs
    fill_late(domains, adjacency_ref.shape[0], late, pool_ref)

    @pl.loop(0, out_ref.shape[0])
    def _(i):
        out_ref[i] = sum_row(slots_ref[i], table_ref, adjacency_ref, pool_ref)


def staying_sum_kernel(table_ref, slots_ref, adjacency_ref, pool_ref, out_ref):
    @pl.loop(0, out_ref.shape[0])
    def _(r):
        @pl.when((r != slots_ref[0]) & (r != slots_ref[1]))
        def _():
            out_ref[r] = sum_row(r, table_ref, adjacency_ref, pool_ref)


def dense_kernel(feats, weight_one_ref, weight_two_ref, *refs):
    parts, outs, hidden_ref = refs[:feats], refs[feats : 2 * feats], refs[2 * feats]
    feat = lax.axis_index("feat")
    width = parts[0].shape[2]
    columns = weight_one_ref.shape[1]
    rows = [part[0] for part in parts]
    for c in range(0, columns, width):
        total = None
        for j in range(feats):
            start = pl.multiple_of((feat ^ j) * width, width)
            part = jnp.dot(
                rows[j],
                weight_one_ref[pl.ds(start, width), c : c + width],
                preferred_element_type=F32,
            )
            total = part if total is None else total + part
        hidden_ref[:, c : c + width] = jnp.maximum(total, 0.0).astype(BF16)
    for j in range(feats):
        start = pl.multiple_of((feat ^ j) * width, width)
        outs[j][0] = jnp.dot(
            hidden_ref[...],
            weight_two_ref[:, pl.ds(start, width)],
            preferred_element_type=F32,
        ).astype(BF16)


def second_pair_kernel(*refs):
    *blocks, pair_ref = refs
    feat = lax.axis_index("feat")
    for j, ref in enumerate(blocks):

        @pl.when((feat ^ j) < 2)
        def _(j=j, ref=ref):
            pair_ref[feat ^ j] = ref[0]


def second_kernel(domains, feats, slots_ref, deal_ref, *refs):
    half = domains // 2
    n_blocks = len(refs) - 1 - (domains - 1)
    blocks, own_ref, sends = refs[:n_blocks], refs[n_blocks], refs[n_blocks + 1 :]
    feat = lax.axis_index("feat")
    for n, ref in enumerate(blocks):
        i, j = divmod(n, feats)
        own_ref[deal_ref[i * feats + (feat ^ j)]] = ref[0]
    write_sends(domains, slots_ref, own_ref, sends[: half - 1], sends[half - 1 :])


def place_kernel(slots_ref, moved_ref, out_in_ref, out_ref, sems):
    del out_in_ref
    copies = [
        pltpu.make_async_copy(moved_ref.at[i], out_ref.at[slots_ref[i]], sems.at[i])
        for i in range(moved_ref.shape[0])
    ]
    for copy in copies:
        copy.start()
    for copy in copies:
        copy.wait()


def call(body, out_shape, in_specs, out_specs, scratch=(), flops=0, moved=0, **kwargs):
    run = pl.pallas_call(
        body,
        out_shape=out_shape,
        in_specs=in_specs,
        out_specs=out_specs,
        scratch_shapes=list(scratch),
        cost_estimate=pl.CostEstimate(flops=flops, bytes_accessed=moved, transcendentals=0),
        compiler_params=pltpu.CompilerParams(vmem_limit_bytes=16 << 20),
        **kwargs,
    )

    def place_and_run(*args):
        placed = [
            a if spec is ANY else pltpu.with_memory_space_constraint(a, spec.memory_space)
            for a, spec in zip(args, in_specs, strict=True)
        ]
        return run(*placed)

    return place_and_run


def exchange(domains, own, pair, sends, which):
    half = domains // 2
    shape = pair.shape[1:]
    near, far = sends[: half - 1], sends[half - 1 :]
    pair = swap(pair, "dom", half)
    near = [swap(near[k - 1], "dom", k) for k in range(1, half)]
    far = [swap(far[k - half], "dom", k) for k in range(half, domains)]
    relay = call(
        functools.partial(relay_kernel, half),
        [block((1, *shape))] * (half - 1),
        [SMEM, VMEM],
        [VMEM] * (half - 1),
        moved=4 * pair.size * half,
    )(which, pair)
    relay = [swap(relay[k - 1], "dom", k) for k in range(1, half)]
    early = [pair, *near, far[0], *far[2:]]
    pool = call(
        functools.partial(fill_early_kernel, domains),
        [block((own.shape[0] + 2 * domains, *shape))],
        [VMEM] * (1 + len(early)),
        [VMEM],
        moved=8 * own.size,
    )(own, *early)[0]
    return [pool, far[1], *relay]


def on_device(features, adjacency, tile_src, mig_slot, weight_one, weight_two):
    domains = lax.axis_size("dom")
    feats = lax.axis_size("feat")
    half = domains // 2
    rows, tiles, size, _ = adjacency.shape
    width = features.shape[1]
    per = rows // feats
    blocks = features.reshape(rows, size, width)
    named, leaving_slots = tile_src.T, mig_slot.T
    near_far = [block((2, size, width))] * (half - 1) + [block((1, size, width))] * half
    pool = block((rows + 2 * domains, size, width))
    work = 2 * tiles * size * size * width
    read = adjacency.size * 2 // rows
    named, mig, own, pair = call(
        load_kernel,
        [
            block(named.shape, I32),
            scalars(leaving_slots.shape),
            block((rows, size, width)),
            block((2, size, width)),
        ],
        [HBM, HBM, HBM],
        [VMEM, SMEM, VMEM, VMEM],
        [pltpu.SemaphoreType.DMA((3,))],
        moved=features.size * 2,
    )(named, leaving_slots, blocks)
    slots, which, deal, *sends = call(
        functools.partial(first_kernel, domains, rows),
        [scalars((2 * domains,)), scalars((domains,)), scalars((rows + 1,)), *near_far],
        [SMEM, VMEM, VMEM],
        [SMEM] * 3 + [VMEM] * len(near_far),
        moved=8 * size * width * domains,
    )(mig, named, own)
    arrived = exchange(domains, own, pair, sends, which)
    loaded = (adjacency, weight_one, weight_two)
    table, adjacency, weight_one, weight_two = call(
        functools.partial(table_kernel, domains, rows),
        [scalars(named.shape)] + [block(x.shape) for x in loaded],
        [SMEM, VMEM, HBM, HBM, HBM],
        [SMEM, VMEM, VMEM, VMEM],
        [pltpu.VMEM(named.shape, I32), pltpu.SemaphoreType.DMA((4,))],
        moved=sum(x.size for x in loaded) * 2,
    )(mig, named, *loaded)

    one = block((1, size, width))
    crossing = [(i, j) for i in range(per) for j in range(2, feats)]
    parts = {}
    pool_one, parts[crossing[0]] = call(
        functools.partial(first_sum_kernel, domains, feats, crossing[0]),
        [pool, one],
        [SMEM, SMEM] + [VMEM] * (1 + len(arrived)),
        [VMEM] * 2,
        flops=work,
        moved=read,
        input_output_aliases={3: 0},
    )(table, deal, adjacency, *arrived)
    for group in [[part] for part in crossing[1:]] + [[(i, 1), (i, 0)] for i in range(per)]:
        outs = call(
            functools.partial(part_sum_kernel, feats, group),
            [one] * len(group),
            [SMEM, SMEM, VMEM, VMEM],
            [VMEM] * len(group),
            flops=work * len(group),
            moved=read * len(group),
        )(table, deal, adjacency, pool_one)
        parts.update(zip(group, outs))
    parts = {(i, j): p if j == 0 else swap(p, "feat", j) for (i, j), p in parts.items()}
    columns = []
    for i in range(per):
        outs = call(
            functools.partial(dense_kernel, feats),
            [one] * feats,
            [VMEM] * (2 + feats),
            [VMEM] * feats,
            [pltpu.VMEM((size, weight_one.shape[1]), BF16)],
            flops=4 * size * weight_one.size,
            moved=weight_one.size * 4,
        )(weight_one, weight_two, *[parts[i, j] for j in range(feats)])
        columns += [c if j == 0 else swap(c, "feat", j) for j, c in enumerate(outs)]

    pair = call(
        second_pair_kernel,
        [block((2, size, width))],
        [VMEM] * feats,
        [VMEM],
        moved=8 * size * width,
    )(*columns[:feats])[0]
    own, *sends = call(
        functools.partial(second_kernel, domains, feats),
        [block((rows, size, width)), *near_far],
        [SMEM, SMEM] + [VMEM] * len(columns),
        [VMEM] * (1 + len(near_far)),
        moved=8 * size * width * domains,
    )(slots, deal, *columns)
    arrived = exchange(domains, own, pair, sends, which)

    pool_two, leaving = call(
        functools.partial(leaving_sum_kernel, domains),
        [pool, block((2, size, width))],
        [SMEM, SMEM] + [VMEM] * (1 + len(arrived)),
        [VMEM] * 2,
        flops=work * 2,
        moved=read * 2,
        input_output_aliases={3: 0},
    )(table, slots, adjacency, *arrived)
    moved = lax.ppermute(leaving, "dom", [(i, (i + 1) % domains) for i in range(domains)])
    out = call(
        staying_sum_kernel,
        jax.ShapeDtypeStruct((rows, size, width), BF16),
        [SMEM, SMEM, VMEM, VMEM],
        VMEM,
        flops=work * (rows - 2),
        moved=read * (rows - 2),
    )(table, slots, adjacency, pool_two)
    out = call(
        place_kernel,
        jax.ShapeDtypeStruct((rows, size, width), BF16),
        [SMEM, VMEM, ANY],
        ANY,
        [pltpu.SemaphoreType.DMA((2,))],
        moved=4 * size * width * 2,
        input_output_aliases={2: 0},
    )(slots, moved, out)
    return out.reshape(rows * size, width)


def solution(mesh):
    in_specs = (P("dom", "feat"), P("dom", None, None, None), P(), P(), P(), P())
    return jax.shard_map(
        on_device, mesh=mesh, in_specs=in_specs, out_specs=P("dom", "feat"), check_vma=False
    )
```

profile of v0, /device:TPU:0, one launch (start us, length us, event | category | flops | bytes accessed | tf_op | source)
XLA Modules:
  0.0 82.1 jit_solution(538063801374210925)
XLA Ops:
  0.0 1.1 %shard_map.64 = (s32[16,64]{1,0:T(8,128)S(1)}, s32[2,8]{1,0:T(2,128)S(4)}, bf16[8,128,256]{2,1,0:T(8,128)(2,1)S(1)}, bf16[2,128,256]{2,1,0:T(8,128)(2,1)S(1)}) custom-call(s32[16,64]{1,0:T(8,128)} %bitcast.5, s32[2,8]{1,0:T(2,128)} %bitcast.6, bf16[8,128,256]{2,1,0:T(8,128)(2,1)} %bitcast.4), custom_call_target="tpu_custom_call" | custom-call | bytes 524288 | tf_op jit(solution)/shard_map/pallas_call | solution.py:274
  1.1 4.1 %collective-permute-start = (bf16[2,128,256]{2,1,0:T(8,128)(2,1)S(1)}, bf16[2,128,256]{2,1,0:T(8,128)(2,1)S(1)}, u32[]{:S(2)}, u32[]{:S(2)}) collective-permute-start(bf16[2,128,256]{2,1,0:T(8,128)(2,1)S(1)} %get-tuple-element.62), channel_id=1, source_target_pairs={{0,16},{4,20},{8,24},{12,28},{16,0},{20,4},{24,8},{28,12},{1,17},{... | collective-permute-start | bytes 393224 | tf_op jit(solution)/shard_map/ppermute | solution.py:21
  5.2 0.3 shard_map.65
  5.6 1.8 %collective-permute-start.1 = (bf16[2,128,256]{2,1,0:T(8,128)(2,1)S(1)}, bf16[2,128,256]{2,1,0:T(8,128)(2,1)S(1)}, u32[]{:S(2)}, u32[]{:S(2)}) collective-permute-start(bf16[2,128,256]{2,1,0:T(8,128)(2,1)S(1)} %get-tuple-element.63), channel_id=1, source_target_pairs={{0,4},{4,0},{8,12},{12,8},{16,20},{20,16},{24,28},{28,24},{1,5},{5... | collective-permute-start | bytes 393224 | tf_op jit(solution)/shard_map/ppermute | solution.py:21
  7.4 1.6 %collective-permute-start.2 = (bf16[2,128,256]{2,1,0:T(8,128)(2,1)S(1)}, bf16[2,128,256]{2,1,0:T(8,128)(2,1)S(1)}, u32[]{:S(2)}, u32[]{:S(2)}) collective-permute-start(bf16[2,128,256]{2,1,0:T(8,128)(2,1)S(1)} %get-tuple-element.64), channel_id=1, source_target_pairs={{0,8},{4,12},{8,0},{12,4},{16,24},{20,28},{24,16},{28,20},{1,9},{5... | collective-permute-start | bytes 393224 | tf_op jit(solution)/shard_map/ppermute | solution.py:21
  9.0 2.5 %collective-permute-start.5 = (bf16[1,128,256]{2,1,0:T(8,128)(2,1)S(1)}, bf16[1,128,256]{2,1,0:T(8,128)(2,1)S(1)}, u32[]{:S(2)}, u32[]{:S(2)}) collective-permute-start(bf16[1,128,256]{2,1,0:T(8,128)(2,1)S(1)} %get-tuple-element.67), channel_id=1, source_target_pairs={{0,24},{4,28},{8,16},{12,20},{16,8},{20,12},{24,0},{28,4},{1,25},{... | collective-permute-start | bytes 196616 | tf_op jit(solution)/shard_map/ppermute | solution.py:21
  11.5 5.0 %collective-permute-done.4.refs_4_ = bf16[1,128,256]{2,1,0:T(8,128)(2,1)S(1)} collective-permute-done((bf16[1,128,256]{2,1,0:T(8,128)(2,1)S(1)}, bf16[1,128,256]{2,1,0:T(8,128)(2,1)S(1)}, u32[]{:S(2)}, u32[]{:S(2)}) %collective-permute-start.4) | collective-permute-done | bytes 65568 | tf_op jit(solution)/shard_map/ppermute | solution.py:21
  16.5 3.9 %collective-permute-start.6 = (bf16[1,128,256]{2,1,0:T(8,128)(2,1)S(1)}, bf16[1,128,256]{2,1,0:T(8,128)(2,1)S(1)}, u32[]{:S(2)}, u32[]{:S(2)}) collective-permute-start(bf16[1,128,256]{2,1,0:T(8,128)(2,1)S(1)} %get-tuple-element.68), channel_id=1, source_target_pairs={{0,28},{4,24},{8,20},{12,16},{16,12},{20,8},{24,4},{28,0},{1,29},{... | collective-permute-start | bytes 196616 | tf_op jit(solution)/shard_map/ppermute | solution.py:21
  20.4 2.4 %collective-permute-start.7 = (bf16[1,128,256]{2,1,0:T(8,128)(2,1)S(1)}, bf16[1,128,256]{2,1,0:T(8,128)(2,1)S(1)}, u32[]{:S(2)}, u32[]{:S(2)}) collective-permute-start(bf16[1,128,256]{2,1,0:T(8,128)(2,1)S(1)} %get-tuple-element.69), channel_id=1, source_target_pairs={{0,20},{4,16},{8,28},{12,24},{16,4},{20,0},{24,12},{28,8},{1,21},{... | collective-permute-start | bytes 196616 | tf_op jit(solution)/shard_map/ppermute | solution.py:21
  22.8 1.2 %collective-permute-done.6.refs_6_ = bf16[1,128,256]{2,1,0:T(8,128)(2,1)S(1)} collective-permute-done((bf16[1,128,256]{2,1,0:T(8,128)(2,1)S(1)}, bf16[1,128,256]{2,1,0:T(8,128)(2,1)S(1)}, u32[]{:S(2)}, u32[]{:S(2)}) %collective-permute-start.6) | collective-permute-done | bytes 65568 | tf_op jit(solution)/shard_map/ppermute | solution.py:21
  24.0 1.0 %collective-permute-start.8 = (bf16[1,128,256]{2,1,0:T(8,128)(2,1)S(1)}, bf16[1,128,256]{2,1,0:T(8,128)(2,1)S(1)}, u32[]{:S(2)}, u32[]{:S(2)}) collective-permute-start(bf16[1,128,256]{2,1,0:T(8,128)(2,1)S(1)} %get-tuple-element.71), channel_id=1, source_target_pairs={{0,4},{4,0},{8,12},{12,8},{16,20},{20,16},{24,28},{28,24},{1,5},{5... | collective-permute-start | bytes 196616 | tf_op jit(solution)/shard_map/ppermute | solution.py:21
  25.1 2.4 %collective-permute-start.10 = (bf16[1,128,256]{2,1,0:T(8,128)(2,1)S(1)}, bf16[1,128,256]{2,1,0:T(8,128)(2,1)S(1)}, u32[]{:S(2)}, u32[]{:S(2)}) collective-permute-start(bf16[1,128,256]{2,1,0:T(8,128)(2,1)S(1)} %get-tuple-element.73), channel_id=1, source_target_pairs={{0,12},{4,8},{8,4},{12,0},{16,28},{20,24},{24,20},{28,16},{1,13},{... | collective-permute-start | bytes 196616 | tf_op jit(solution)/shard_map/ppermute | solution.py:21
  27.5 3.5 %shard_map.66 = (s32[16,64]{1,0:T(8,128)S(4)}, bf16[8,16,128,128]{3,2,1,0:T(8,128)(2,1)S(1)}, bf16[1024,1024]{1,0:T(8,128)(2,1)S(1)}, bf16[1024,1024]{1,0:T(8,128)(2,1)S(1)}) custom-call(s32[2,8]{1,0:T(2,128)S(4)} %get-tuple-element.53.mig, s32[16,64]{1,0:T(8,128)S(1)} %get-tuple-element.54.tiles_ref, bf16[8,16,128,128]{3,2,1,0:T(8,128)(2,1)} %refs_0_.1, ...), custom_call_target="tpu_custom_call" | custom-call | bytes 8388608 | tf_op jit(solution)/shard_map/pallas_call | solution.py:274
  31.2 0.4 shard_map.69
  31.6 0.5 shard_map.70
  32.1 0.3 shard_map.71
  32.5 1.6 %collective-permute-start.12 = (bf16[1,128,256]{2,1,0:T(8,128)(2,1)S(1)}, bf16[1,128,256]{2,1,0:T(8,128)(2,1)S(1)}, u32[]{:S(2)}, u32[]{:S(2)}) collective-permute-start(bf16[1,128,256]{2,1,0:T(8,128)(2,1)S(1)} %get-tuple-element.77), channel_id=1, source_target_pairs={{0,2},{1,3},{2,0},{3,1},{4,6},{5,7},{6,4},{7,5},{8,10},{9,11},{10,... | collective-permute-start | bytes 196616 | tf_op jit(solution)/shard_map/ppermute | solution.py:21
  34.3 0.5 shard_map.73
  34.8 0.4 collective-permute-start.17
  35.3 0.3 shard_map.74
  35.6 1.6 %collective-permute-start.18 = (bf16[1,128,256]{2,1,0:T(8,128)(2,1)S(1)}, bf16[1,128,256]{2,1,0:T(8,128)(2,1)S(1)}, u32[]{:S(2)}, u32[]{:S(2)}) collective-permute-start(bf16[1,128,256]{2,1,0:T(8,128)(2,1)S(1)} %shard_map.74), channel_id=1, source_target_pairs={{0,2},{1,3},{2,0},{3,1},{4,6},{5,7},{6,4},{7,5},{8,10},{9,11},{10,... | collective-permute-start | bytes 196616 | tf_op jit(solution)/shard_map/ppermute | solution.py:21
  37.2 0.3 shard_map.75
  37.6 0.5 collective-permute-done.13.refs_3_
  38.1 0.8 shard_map.72
  39.2 1.4 %collective-permute-start.15 = (bf16[1,128,256]{2,1,0:T(8,128)(2,1)S(1)}, bf16[1,128,256]{2,1,0:T(8,128)(2,1)S(1)}, u32[]{:S(2)}, u32[]{:S(2)}) collective-permute-start(bf16[1,128,256]{2,1,0:T(8,128)(2,1)S(1)} %get-tuple-element.80), channel_id=1, source_target_pairs={{0,2},{1,3},{2,0},{3,1},{4,6},{5,7},{6,4},{7,5},{8,10},{9,11},{10,... | collective-permute-start | bytes 196616 | tf_op jit(solution)/shard_map/ppermute | solution.py:21
  40.9 1.1 %collective-permute-done.19.refs_3_ = bf16[1,128,256]{2,1,0:T(8,128)(2,1)S(1)} collective-permute-done((bf16[1,128,256]{2,1,0:T(8,128)(2,1)S(1)}, bf16[1,128,256]{2,1,0:T(8,128)(2,1)S(1)}, u32[]{:S(2)}, u32[]{:S(2)}) %collective-permute-start.19) | collective-permute-done | bytes 65568 | tf_op jit(solution)/shard_map/ppermute | solution.py:21
  41.9 0.8 shard_map.76
  42.9 0.7 collective-permute-start.21
  43.6 1.0 %collective-permute-start.22 = (bf16[1,128,256]{2,1,0:T(8,128)(2,1)S(1)}, bf16[1,128,256]{2,1,0:T(8,128)(2,1)S(1)}, u32[]{:S(2)}, u32[]{:S(2)}) collective-permute-start(bf16[1,128,256]{2,1,0:T(8,128)(2,1)S(1)} %get-tuple-element.87), channel_id=1, source_target_pairs={{0,3},{1,2},{2,1},{3,0},{4,7},{5,6},{6,5},{7,4},{8,11},{9,10},{10,... | collective-permute-start | bytes 196616 | tf_op jit(solution)/shard_map/ppermute | solution.py:21
  44.6 0.3 collective-permute-done.16.refs_3_
  45.0 3.2 %collective-permute-start.23 = (bf16[2,128,256]{2,1,0:T(8,128)(2,1)S(1)}, bf16[2,128,256]{2,1,0:T(8,128)(2,1)S(1)}, u32[]{:S(2)}, u32[]{:S(2)}) collective-permute-start(bf16[2,128,256]{2,1,0:T(8,128)(2,1)S(1)} %shard_map.78), channel_id=1, source_target_pairs={{0,16},{4,20},{8,24},{12,28},{16,0},{20,4},{24,8},{28,12},{1,17},{... | collective-permute-start | bytes 393224 | tf_op jit(solution)/shard_map/ppermute | solution.py:21
  48.3 3.1 %collective-permute-start.27 = (bf16[1,128,256]{2,1,0:T(8,128)(2,1)S(1)}, bf16[1,128,256]{2,1,0:T(8,128)(2,1)S(1)}, u32[]{:S(2)}, u32[]{:S(2)}) collective-permute-start(bf16[1,128,256]{2,1,0:T(8,128)(2,1)S(1)} %get-tuple-element.92), channel_id=1, source_target_pairs={{0,16},{4,20},{8,24},{12,28},{16,0},{20,4},{24,8},{28,12},{1,17},{... | collective-permute-start | bytes 196616 | tf_op jit(solution)/shard_map/ppermute | solution.py:21
  51.5 0.6 collective-permute-start.24
  52.1 1.4 %collective-permute-start.25 = (bf16[2,128,256]{2,1,0:T(8,128)(2,1)S(1)}, bf16[2,128,256]{2,1,0:T(8,128)(2,1)S(1)}, u32[]{:S(2)}, u32[]{:S(2)}) collective-permute-start(bf16[2,128,256]{2,1,0:T(8,128)(2,1)S(1)} %get-tuple-element.90), channel_id=1, source_target_pairs={{0,8},{4,12},{8,0},{12,4},{16,24},{20,28},{24,16},{28,20},{1,9},{5... | collective-permute-start | bytes 393224 | tf_op jit(solution)/shard_map/ppermute | solution.py:21
  53.7 4.7 %collective-permute-done.27.refs_4_ = bf16[1,128,256]{2,1,0:T(8,128)(2,1)S(1)} collective-permute-done((bf16[1,128,256]{2,1,0:T(8,128)(2,1)S(1)}, bf16[1,128,256]{2,1,0:T(8,128)(2,1)S(1)}, u32[]{:S(2)}, u32[]{:S(2)}) %collective-permute-start.27) | collective-permute-done | bytes 65568 | tf_op jit(solution)/shard_map/ppermute | solution.py:21
  58.5 4.3 %collective-permute-start.29 = (bf16[1,128,256]{2,1,0:T(8,128)(2,1)S(1)}, bf16[1,128,256]{2,1,0:T(8,128)(2,1)S(1)}, u32[]{:S(2)}, u32[]{:S(2)}) collective-permute-start(bf16[1,128,256]{2,1,0:T(8,128)(2,1)S(1)} %get-tuple-element.94), channel_id=1, source_target_pairs={{0,28},{4,24},{8,20},{12,16},{16,12},{20,8},{24,4},{28,0},{1,29},{... | collective-permute-start | bytes 196616 | tf_op jit(solution)/shard_map/ppermute | solution.py:21
  62.8 2.4 %collective-permute-start.30 = (bf16[1,128,256]{2,1,0:T(8,128)(2,1)S(1)}, bf16[1,128,256]{2,1,0:T(8,128)(2,1)S(1)}, u32[]{:S(2)}, u32[]{:S(2)}) collective-permute-start(bf16[1,128,256]{2,1,0:T(8,128)(2,1)S(1)} %get-tuple-element.95), channel_id=1, source_target_pairs={{0,20},{4,16},{8,28},{12,24},{16,4},{20,0},{24,12},{28,8},{1,21},{... | collective-permute-start | bytes 196616 | tf_op jit(solution)/shard_map/ppermute | solution.py:21
  65.2 0.9 %collective-permute-done.29.refs_6_ = bf16[1,128,256]{2,1,0:T(8,128)(2,1)S(1)} collective-permute-done((bf16[1,128,256]{2,1,0:T(8,128)(2,1)S(1)}, bf16[1,128,256]{2,1,0:T(8,128)(2,1)S(1)}, u32[]{:S(2)}, u32[]{:S(2)}) %collective-permute-start.29) | collective-permute-done | bytes 65568 | tf_op jit(solution)/shard_map/ppermute | solution.py:21
  66.1 1.2 %collective-permute-start.31 = (bf16[1,128,256]{2,1,0:T(8,128)(2,1)S(1)}, bf16[1,128,256]{2,1,0:T(8,128)(2,1)S(1)}, u32[]{:S(2)}, u32[]{:S(2)}) collective-permute-start(bf16[1,128,256]{2,1,0:T(8,128)(2,1)S(1)} %get-tuple-element.96), channel_id=1, source_target_pairs={{0,4},{4,0},{8,12},{12,8},{16,20},{20,16},{24,28},{28,24},{1,5},{5... | collective-permute-start | bytes 196616 | tf_op jit(solution)/shard_map/ppermute | solution.py:21
  67.4 2.3 %collective-permute-start.33 = (bf16[1,128,256]{2,1,0:T(8,128)(2,1)S(1)}, bf16[1,128,256]{2,1,0:T(8,128)(2,1)S(1)}, u32[]{:S(2)}, u32[]{:S(2)}) collective-permute-start(bf16[1,128,256]{2,1,0:T(8,128)(2,1)S(1)} %get-tuple-element.98), channel_id=1, source_target_pairs={{0,12},{4,8},{8,4},{12,0},{16,28},{20,24},{24,20},{28,16},{1,13},{... | collective-permute-start | bytes 196616 | tf_op jit(solution)/shard_map/ppermute | solution.py:21
  69.6 1.6 %collective-permute-done.26.refs_3_ = bf16[2,128,256]{2,1,0:T(8,128)(2,1)S(1)} collective-permute-done((bf16[2,128,256]{2,1,0:T(8,128)(2,1)S(1)}, bf16[2,128,256]{2,1,0:T(8,128)(2,1)S(1)}, u32[]{:S(2)}, u32[]{:S(2)}) %collective-permute-start.26) | collective-permute-done | bytes 131104 | tf_op jit(solution)/shard_map/ppermute | solution.py:21
  71.3 1.0 %collective-permute-done.31.refs_2_ = bf16[1,128,256]{2,1,0:T(8,128)(2,1)S(1)} collective-permute-done((bf16[1,128,256]{2,1,0:T(8,128)(2,1)S(1)}, bf16[1,128,256]{2,1,0:T(8,128)(2,1)S(1)}, u32[]{:S(2)}, u32[]{:S(2)}) %collective-permute-start.31) | collective-permute-done | bytes 65568 | tf_op jit(solution)/shard_map/ppermute | solution.py:21
  72.3 0.7 collective-permute-done.33.refs_4_
  73.0 0.7 shard_map.81
  73.7 0.9 %collective-permute-start.34 = (bf16[2,128,256]{2,1,0:T(8,128)(2,1)S(1)}, bf16[2,128,256]{2,1,0:T(8,128)(2,1)S(1)}, u32[]{:S(2)}, u32[]{:S(2)}) collective-permute-start(bf16[2,128,256]{2,1,0:T(8,128)(2,1)S(1)} %get-tuple-element.99), channel_id=1, source_target_pairs={{0,4},{4,8},{8,12},{12,16},{16,20},{20,24},{24,28},{28,0},{1,5},{5... | collective-permute-start | bytes 393224 | tf_op jit(solution)/shard_map/ppermute | solution.py:410
  74.6 2.9 %shard_map.82.out_in_ref = bf16[8,128,256]{2,1,0:T(8,128)(2,1)} custom-call(s32[16,64]{1,0:T(8,128)S(4)} %get-tuple-element.57.table_ref, s32[16]{0:T(128)S(4)} %get-tuple-element.56.slots_ref, bf16[8,16,128,128]{3,2,1,0:T(8,128)(2,1)S(1)} %get-tuple-element.58.adjacency_ref, bf16[24,128,256]{2,1,0:T(8,128)(2,1)S(1)} %get-tuple-element.100.pool_ref), custom_call_target="tpu_custom_call" | custom-call | flops 805306368 | bytes 3145728 | tf_op jit(solution)/shard_map/pallas_call | solution.py:274
  77.5 3.9 %collective-permute-done.34.moved_ref = bf16[2,128,256]{2,1,0:T(8,128)(2,1)S(1)} collective-permute-done((bf16[2,128,256]{2,1,0:T(8,128)(2,1)S(1)}, bf16[2,128,256]{2,1,0:T(8,128)(2,1)S(1)}, u32[]{:S(2)}, u32[]{:S(2)}) %collective-permute-start.34) | collective-permute-done | bytes 131104 | tf_op jit(solution)/shard_map/ppermute | solution.py:410
  81.4 0.7 shard_map.83
  (42 shorter events, 1.9 us)
Async XLA Ops:
  1.1 19.3 %collective-permute-start = (bf16[2,128,256]{2,1,0:T(8,128)(2,1)S(1)}, bf16[2,128,256]{2,1,0:T(8,128)(2,1)S(1)}, u32[]{:S(2)}, u32[]{:S(2)}) collective-permute-start(bf16[2,128,256]{2,1,0:T(8,128)(2,1)S(1)} %get-tuple-element.62), channel_id=1, source_target_pairs={{0,16},{4,20},{8,24},{12,28},{16,0},{20,4},{24,8},{28,12},{1,17},{... | collective-permute-start | bytes 393224 | tf_op jit(solution)/shard_map/ppermute | solution.py:21
  5.5 10.9 %collective-permute-start.4 = (bf16[1,128,256]{2,1,0:T(8,128)(2,1)S(1)}, bf16[1,128,256]{2,1,0:T(8,128)(2,1)S(1)}, u32[]{:S(2)}, u32[]{:S(2)}) collective-permute-start(bf16[1,128,256]{2,1,0:T(8,128)(2,1)S(1)} %get-tuple-element.66), channel_id=1, source_target_pairs={{0,16},{4,20},{8,24},{12,28},{16,0},{20,4},{24,8},{28,12},{1,17},{... | collective-permute-start | bytes 196616 | tf_op jit(solution)/shard_map/ppermute | solution.py:21
  5.6 19.5 %collective-permute-start.1 = (bf16[2,128,256]{2,1,0:T(8,128)(2,1)S(1)}, bf16[2,128,256]{2,1,0:T(8,128)(2,1)S(1)}, u32[]{:S(2)}, u32[]{:S(2)}) collective-permute-start(bf16[2,128,256]{2,1,0:T(8,128)(2,1)S(1)} %get-tuple-element.63), channel_id=1, source_target_pairs={{0,4},{4,0},{8,12},{12,8},{16,20},{20,16},{24,28},{28,24},{1,5},{5... | collective-permute-start | bytes 393224 | tf_op jit(solution)/shard_map/ppermute | solution.py:21
  7.4 17.7 %collective-permute-start.2 = (bf16[2,128,256]{2,1,0:T(8,128)(2,1)S(1)}, bf16[2,128,256]{2,1,0:T(8,128)(2,1)S(1)}, u32[]{:S(2)}, u32[]{:S(2)}) collective-permute-start(bf16[2,128,256]{2,1,0:T(8,128)(2,1)S(1)} %get-tuple-element.64), channel_id=1, source_target_pairs={{0,8},{4,12},{8,0},{12,4},{16,24},{20,28},{24,16},{28,20},{1,9},{5... | collective-permute-start | bytes 393224 | tf_op jit(solution)/shard_map/ppermute | solution.py:21
  9.0 11.4 %collective-permute-start.5 = (bf16[1,128,256]{2,1,0:T(8,128)(2,1)S(1)}, bf16[1,128,256]{2,1,0:T(8,128)(2,1)S(1)}, u32[]{:S(2)}, u32[]{:S(2)}) collective-permute-start(bf16[1,128,256]{2,1,0:T(8,128)(2,1)S(1)} %get-tuple-element.67), channel_id=1, source_target_pairs={{0,24},{4,28},{8,16},{12,20},{16,8},{20,12},{24,0},{28,4},{1,25},{... | collective-permute-start | bytes 196616 | tf_op jit(solution)/shard_map/ppermute | solution.py:21
  16.5 7.6 %collective-permute-start.6 = (bf16[1,128,256]{2,1,0:T(8,128)(2,1)S(1)}, bf16[1,128,256]{2,1,0:T(8,128)(2,1)S(1)}, u32[]{:S(2)}, u32[]{:S(2)}) collective-permute-start(bf16[1,128,256]{2,1,0:T(8,128)(2,1)S(1)} %get-tuple-element.68), channel_id=1, source_target_pairs={{0,28},{4,24},{8,20},{12,16},{16,12},{20,8},{24,4},{28,0},{1,29},{... | collective-permute-start | bytes 196616 | tf_op jit(solution)/shard_map/ppermute | solution.py:21
  20.4 10.7 %collective-permute-start.3 = (bf16[2,128,256]{2,1,0:T(8,128)(2,1)S(1)}, bf16[2,128,256]{2,1,0:T(8,128)(2,1)S(1)}, u32[]{:S(2)}, u32[]{:S(2)}) collective-permute-start(bf16[2,128,256]{2,1,0:T(8,128)(2,1)S(1)} %get-tuple-element.65), channel_id=1, source_target_pairs={{0,12},{4,8},{8,4},{12,0},{16,28},{20,24},{24,20},{28,16},{1,13},{... | collective-permute-start | bytes 393224 | tf_op jit(solution)/shard_map/ppermute | solution.py:21
  20.4 10.8 %collective-permute-start.7 = (bf16[1,128,256]{2,1,0:T(8,128)(2,1)S(1)}, bf16[1,128,256]{2,1,0:T(8,128)(2,1)S(1)}, u32[]{:S(2)}, u32[]{:S(2)}) collective-permute-start(bf16[1,128,256]{2,1,0:T(8,128)(2,1)S(1)} %get-tuple-element.69), channel_id=1, source_target_pairs={{0,20},{4,16},{8,28},{12,24},{16,4},{20,0},{24,12},{28,8},{1,21},{... | collective-permute-start | bytes 196616 | tf_op jit(solution)/shard_map/ppermute | solution.py:21
  24.0 7.1 %collective-permute-start.8 = (bf16[1,128,256]{2,1,0:T(8,128)(2,1)S(1)}, bf16[1,128,256]{2,1,0:T(8,128)(2,1)S(1)}, u32[]{:S(2)}, u32[]{:S(2)}) collective-permute-start(bf16[1,128,256]{2,1,0:T(8,128)(2,1)S(1)} %get-tuple-element.71), channel_id=1, source_target_pairs={{0,4},{4,0},{8,12},{12,8},{16,20},{20,16},{24,28},{28,24},{1,5},{5... | collective-permute-start | bytes 196616 | tf_op jit(solution)/shard_map/ppermute | solution.py:21
  25.1 6.1 %collective-permute-start.9 = (bf16[1,128,256]{2,1,0:T(8,128)(2,1)S(1)}, bf16[1,128,256]{2,1,0:T(8,128)(2,1)S(1)}, u32[]{:S(2)}, u32[]{:S(2)}) collective-permute-start(bf16[1,128,256]{2,1,0:T(8,128)(2,1)S(1)} %get-tuple-element.72), channel_id=1, source_target_pairs={{0,8},{4,12},{8,0},{12,4},{16,24},{20,28},{24,16},{28,20},{1,9},{5... | collective-permute-start | bytes 196616 | tf_op jit(solution)/shard_map/ppermute | solution.py:21
  25.1 6.1 %collective-permute-start.10 = (bf16[1,128,256]{2,1,0:T(8,128)(2,1)S(1)}, bf16[1,128,256]{2,1,0:T(8,128)(2,1)S(1)}, u32[]{:S(2)}, u32[]{:S(2)}) collective-permute-start(bf16[1,128,256]{2,1,0:T(8,128)(2,1)S(1)} %get-tuple-element.73), channel_id=1, source_target_pairs={{0,12},{4,8},{8,4},{12,0},{16,28},{20,24},{24,20},{28,16},{1,13},{... | collective-permute-start | bytes 196616 | tf_op jit(solution)/shard_map/ppermute | solution.py:21
  32.4 5.1 %collective-permute-start.11 = (bf16[1,128,256]{2,1,0:T(8,128)(2,1)S(1)}, bf16[1,128,256]{2,1,0:T(8,128)(2,1)S(1)}, u32[]{:S(2)}, u32[]{:S(2)}) collective-permute-start(bf16[1,128,256]{2,1,0:T(8,128)(2,1)S(1)} %get-tuple-element.76), channel_id=1, source_target_pairs={{0,1},{1,0},{2,3},{3,2},{4,5},{5,4},{6,7},{7,6},{8,9},{9,8},{10,11... | collective-permute-start | bytes 196616 | tf_op jit(solution)/shard_map/ppermute | solution.py:21
  32.5 5.1 %collective-permute-start.12 = (bf16[1,128,256]{2,1,0:T(8,128)(2,1)S(1)}, bf16[1,128,256]{2,1,0:T(8,128)(2,1)S(1)}, u32[]{:S(2)}, u32[]{:S(2)}) collective-permute-start(bf16[1,128,256]{2,1,0:T(8,128)(2,1)S(1)} %get-tuple-element.77), channel_id=1, source_target_pairs={{0,2},{1,3},{2,0},{3,1},{4,6},{5,7},{6,4},{7,5},{8,10},{9,11},{10,... | collective-permute-start | bytes 196616 | tf_op jit(solution)/shard_map/ppermute | solution.py:21
  34.1 4.1 %collective-permute-start.13 = (bf16[1,128,256]{2,1,0:T(8,128)(2,1)S(1)}, bf16[1,128,256]{2,1,0:T(8,128)(2,1)S(1)}, u32[]{:S(2)}, u32[]{:S(2)}) collective-permute-start(bf16[1,128,256]{2,1,0:T(8,128)(2,1)S(1)} %shard_map.71), channel_id=1, source_target_pairs={{0,3},{1,2},{2,1},{3,0},{4,7},{5,6},{6,5},{7,4},{8,11},{9,10},{10,... | collective-permute-start | bytes 196616 | tf_op jit(solution)/shard_map/ppermute | solution.py:21
  34.8 5.8 %collective-permute-start.17 = (bf16[1,128,256]{2,1,0:T(8,128)(2,1)S(1)}, bf16[1,128,256]{2,1,0:T(8,128)(2,1)S(1)}, u32[]{:S(2)}, u32[]{:S(2)}) collective-permute-start(bf16[1,128,256]{2,1,0:T(8,128)(2,1)S(1)} %get-tuple-element.83), channel_id=1, source_target_pairs={{0,1},{1,0},{2,3},{3,2},{4,5},{5,4},{6,7},{7,6},{8,9},{9,8},{10,11... | collective-permute-start | bytes 196616 | tf_op jit(solution)/shard_map/ppermute | solution.py:21
  35.6 5.3 %collective-permute-start.18 = (bf16[1,128,256]{2,1,0:T(8,128)(2,1)S(1)}, bf16[1,128,256]{2,1,0:T(8,128)(2,1)S(1)}, u32[]{:S(2)}, u32[]{:S(2)}) collective-permute-start(bf16[1,128,256]{2,1,0:T(8,128)(2,1)S(1)} %shard_map.74), channel_id=1, source_target_pairs={{0,2},{1,3},{2,0},{3,1},{4,6},{5,7},{6,4},{7,5},{8,10},{9,11},{10,... | collective-permute-start | bytes 196616 | tf_op jit(solution)/shard_map/ppermute | solution.py:21
  37.5 4.4 %collective-permute-start.19 = (bf16[1,128,256]{2,1,0:T(8,128)(2,1)S(1)}, bf16[1,128,256]{2,1,0:T(8,128)(2,1)S(1)}, u32[]{:S(2)}, u32[]{:S(2)}) collective-permute-start(bf16[1,128,256]{2,1,0:T(8,128)(2,1)S(1)} %shard_map.75), channel_id=1, source_target_pairs={{0,3},{1,2},{2,1},{3,0},{4,7},{5,6},{6,5},{7,4},{8,11},{9,10},{10,... | collective-permute-start | bytes 196616 | tf_op jit(solution)/shard_map/ppermute | solution.py:21
  38.9 4.7 %collective-permute-start.14 = (bf16[1,128,256]{2,1,0:T(8,128)(2,1)S(1)}, bf16[1,128,256]{2,1,0:T(8,128)(2,1)S(1)}, u32[]{:S(2)}, u32[]{:S(2)}) collective-permute-start(bf16[1,128,256]{2,1,0:T(8,128)(2,1)S(1)} %get-tuple-element.79), channel_id=1, source_target_pairs={{0,1},{1,0},{2,3},{3,2},{4,5},{5,4},{6,7},{7,6},{8,9},{9,8},{10,11... | collective-permute-start | bytes 196616 | tf_op jit(solution)/shard_map/ppermute | solution.py:21
  39.2 5.4 %collective-permute-start.15 = (bf16[1,128,256]{2,1,0:T(8,128)(2,1)S(1)}, bf16[1,128,256]{2,1,0:T(8,128)(2,1)S(1)}, u32[]{:S(2)}, u32[]{:S(2)}) collective-permute-start(bf16[1,128,256]{2,1,0:T(8,128)(2,1)S(1)} %get-tuple-element.80), channel_id=1, source_target_pairs={{0,2},{1,3},{2,0},{3,1},{4,6},{5,7},{6,4},{7,5},{8,10},{9,11},{10,... | collective-permute-start | bytes 196616 | tf_op jit(solution)/shard_map/ppermute | solution.py:21
  40.6 4.4 %collective-permute-start.16 = (bf16[1,128,256]{2,1,0:T(8,128)(2,1)S(1)}, bf16[1,128,256]{2,1,0:T(8,128)(2,1)S(1)}, u32[]{:S(2)}, u32[]{:S(2)}) collective-permute-start(bf16[1,128,256]{2,1,0:T(8,128)(2,1)S(1)} %get-tuple-element.81), channel_id=1, source_target_pairs={{0,3},{1,2},{2,1},{3,0},{4,7},{5,6},{6,5},{7,4},{8,11},{9,10},{10,... | collective-permute-start | bytes 196616 | tf_op jit(solution)/shard_map/ppermute | solution.py:21
  42.7 5.5 %collective-permute-start.20 = (bf16[1,128,256]{2,1,0:T(8,128)(2,1)S(1)}, bf16[1,128,256]{2,1,0:T(8,128)(2,1)S(1)}, u32[]{:S(2)}, u32[]{:S(2)}) collective-permute-start(bf16[1,128,256]{2,1,0:T(8,128)(2,1)S(1)} %get-tuple-element.85), channel_id=1, source_target_pairs={{0,1},{1,0},{2,3},{3,2},{4,5},{5,4},{6,7},{7,6},{8,9},{9,8},{10,11... | collective-permute-start | bytes 196616 | tf_op jit(solution)/shard_map/ppermute | solution.py:21
  42.9 5.3 %collective-permute-start.21 = (bf16[1,128,256]{2,1,0:T(8,128)(2,1)S(1)}, bf16[1,128,256]{2,1,0:T(8,128)(2,1)S(1)}, u32[]{:S(2)}, u32[]{:S(2)}) collective-permute-start(bf16[1,128,256]{2,1,0:T(8,128)(2,1)S(1)} %get-tuple-element.86), channel_id=1, source_target_pairs={{0,2},{1,3},{2,0},{3,1},{4,6},{5,7},{6,4},{7,5},{8,10},{9,11},{10,... | collective-permute-start | bytes 196616 | tf_op jit(solution)/shard_map/ppermute | solution.py:21
  43.6 4.6 %collective-permute-start.22 = (bf16[1,128,256]{2,1,0:T(8,128)(2,1)S(1)}, bf16[1,128,256]{2,1,0:T(8,128)(2,1)S(1)}, u32[]{:S(2)}, u32[]{:S(2)}) collective-permute-start(bf16[1,128,256]{2,1,0:T(8,128)(2,1)S(1)} %get-tuple-element.87), channel_id=1, source_target_pairs={{0,3},{1,2},{2,1},{3,0},{4,7},{5,6},{6,5},{7,4},{8,11},{9,10},{10,... | collective-permute-start | bytes 196616 | tf_op jit(solution)/shard_map/ppermute | solution.py:21
  45.0 17.7 %collective-permute-start.23 = (bf16[2,128,256]{2,1,0:T(8,128)(2,1)S(1)}, bf16[2,128,256]{2,1,0:T(8,128)(2,1)S(1)}, u32[]{:S(2)}, u32[]{:S(2)}) collective-permute-start(bf16[2,128,256]{2,1,0:T(8,128)(2,1)S(1)} %shard_map.78), channel_id=1, source_target_pairs={{0,16},{4,20},{8,24},{12,28},{16,0},{20,4},{24,8},{28,12},{1,17},{... | collective-permute-start | bytes 393224 | tf_op jit(solution)/shard_map/ppermute | solution.py:21
  48.3 10.1 %collective-permute-start.27 = (bf16[1,128,256]{2,1,0:T(8,128)(2,1)S(1)}, bf16[1,128,256]{2,1,0:T(8,128)(2,1)S(1)}, u32[]{:S(2)}, u32[]{:S(2)}) collective-permute-start(bf16[1,128,256]{2,1,0:T(8,128)(2,1)S(1)} %get-tuple-element.92), channel_id=1, source_target_pairs={{0,16},{4,20},{8,24},{12,28},{16,0},{20,4},{24,8},{28,12},{1,17},{... | collective-permute-start | bytes 196616 | tf_op jit(solution)/shard_map/ppermute | solution.py:21
  51.5 15.9 %collective-permute-start.24 = (bf16[2,128,256]{2,1,0:T(8,128)(2,1)S(1)}, bf16[2,128,256]{2,1,0:T(8,128)(2,1)S(1)}, u32[]{:S(2)}, u32[]{:S(2)}) collective-permute-start(bf16[2,128,256]{2,1,0:T(8,128)(2,1)S(1)} %get-tuple-element.89), channel_id=1, source_target_pairs={{0,4},{4,0},{8,12},{12,8},{16,20},{20,16},{24,28},{28,24},{1,5},{5... | collective-permute-start | bytes 393224 | tf_op jit(solution)/shard_map/ppermute | solution.py:21
  52.1 15.3 %collective-permute-start.25 = (bf16[2,128,256]{2,1,0:T(8,128)(2,1)S(1)}, bf16[2,128,256]{2,1,0:T(8,128)(2,1)S(1)}, u32[]{:S(2)}, u32[]{:S(2)}) collective-permute-start(bf16[2,128,256]{2,1,0:T(8,128)(2,1)S(1)} %get-tuple-element.90), channel_id=1, source_target_pairs={{0,8},{4,12},{8,0},{12,4},{16,24},{20,28},{24,16},{28,20},{1,9},{5... | collective-permute-start | bytes 393224 | tf_op jit(solution)/shard_map/ppermute | solution.py:21
  53.4 9.3 %collective-permute-start.28 = (bf16[1,128,256]{2,1,0:T(8,128)(2,1)S(1)}, bf16[1,128,256]{2,1,0:T(8,128)(2,1)S(1)}, u32[]{:S(2)}, u32[]{:S(2)}) collective-permute-start(bf16[1,128,256]{2,1,0:T(8,128)(2,1)S(1)} %get-tuple-element.93), channel_id=1, source_target_pairs={{0,24},{4,28},{8,16},{12,20},{16,8},{20,12},{24,0},{28,4},{1,25},{... | collective-permute-start | bytes 196616 | tf_op jit(solution)/shard_map/ppermute | solution.py:21
  58.5 7.7 %collective-permute-start.29 = (bf16[1,128,256]{2,1,0:T(8,128)(2,1)S(1)}, bf16[1,128,256]{2,1,0:T(8,128)(2,1)S(1)}, u32[]{:S(2)}, u32[]{:S(2)}) collective-permute-start(bf16[1,128,256]{2,1,0:T(8,128)(2,1)S(1)} %get-tuple-element.94), channel_id=1, source_target_pairs={{0,28},{4,24},{8,20},{12,16},{16,12},{20,8},{24,4},{28,0},{1,29},{... | collective-permute-start | bytes 196616 | tf_op jit(solution)/shard_map/ppermute | solution.py:21
  62.7 8.5 %collective-permute-start.26 = (bf16[2,128,256]{2,1,0:T(8,128)(2,1)S(1)}, bf16[2,128,256]{2,1,0:T(8,128)(2,1)S(1)}, u32[]{:S(2)}, u32[]{:S(2)}) collective-permute-start(bf16[2,128,256]{2,1,0:T(8,128)(2,1)S(1)} %get-tuple-element.91), channel_id=1, source_target_pairs={{0,12},{4,8},{8,4},{12,0},{16,28},{20,24},{24,20},{28,16},{1,13},{... | collective-permute-start | bytes 393224 | tf_op jit(solution)/shard_map/ppermute | solution.py:21
  62.8 8.5 %collective-permute-start.30 = (bf16[1,128,256]{2,1,0:T(8,128)(2,1)S(1)}, bf16[1,128,256]{2,1,0:T(8,128)(2,1)S(1)}, u32[]{:S(2)}, u32[]{:S(2)}) collective-permute-start(bf16[1,128,256]{2,1,0:T(8,128)(2,1)S(1)} %get-tuple-element.95), channel_id=1, source_target_pairs={{0,20},{4,16},{8,28},{12,24},{16,4},{20,0},{24,12},{28,8},{1,21},{... | collective-permute-start | bytes 196616 | tf_op jit(solution)/shard_map/ppermute | solution.py:21
  66.1 6.1 %collective-permute-start.31 = (bf16[1,128,256]{2,1,0:T(8,128)(2,1)S(1)}, bf16[1,128,256]{2,1,0:T(8,128)(2,1)S(1)}, u32[]{:S(2)}, u32[]{:S(2)}) collective-permute-start(bf16[1,128,256]{2,1,0:T(8,128)(2,1)S(1)} %get-tuple-element.96), channel_id=1, source_target_pairs={{0,4},{4,0},{8,12},{12,8},{16,20},{20,16},{24,28},{28,24},{1,5},{5... | collective-permute-start | bytes 196616 | tf_op jit(solution)/shard_map/ppermute | solution.py:21
  67.4 4.9 %collective-permute-start.32 = (bf16[1,128,256]{2,1,0:T(8,128)(2,1)S(1)}, bf16[1,128,256]{2,1,0:T(8,128)(2,1)S(1)}, u32[]{:S(2)}, u32[]{:S(2)}) collective-permute-start(bf16[1,128,256]{2,1,0:T(8,128)(2,1)S(1)} %get-tuple-element.97), channel_id=1, source_target_pairs={{0,8},{4,12},{8,0},{12,4},{16,24},{20,28},{24,16},{28,20},{1,9},{5... | collective-permute-start | bytes 196616 | tf_op jit(solution)/shard_map/ppermute | solution.py:21
  67.4 5.6 %collective-permute-start.33 = (bf16[1,128,256]{2,1,0:T(8,128)(2,1)S(1)}, bf16[1,128,256]{2,1,0:T(8,128)(2,1)S(1)}, u32[]{:S(2)}, u32[]{:S(2)}) collective-permute-start(bf16[1,128,256]{2,1,0:T(8,128)(2,1)S(1)} %get-tuple-element.98), channel_id=1, source_target_pairs={{0,12},{4,8},{8,4},{12,0},{16,28},{20,24},{24,20},{28,16},{1,13},{... | collective-permute-start | bytes 196616 | tf_op jit(solution)/shard_map/ppermute | solution.py:21
  73.7 7.7 %collective-permute-start.34 = (bf16[2,128,256]{2,1,0:T(8,128)(2,1)S(1)}, bf16[2,128,256]{2,1,0:T(8,128)(2,1)S(1)}, u32[]{:S(2)}, u32[]{:S(2)}) collective-permute-start(bf16[2,128,256]{2,1,0:T(8,128)(2,1)S(1)} %get-tuple-element.99), channel_id=1, source_target_pairs={{0,4},{4,8},{8,12},{12,16},{16,20},{20,24},{24,28},{28,0},{1,5},{5... | collective-permute-start | bytes 393224 | tf_op jit(solution)/shard_map/ppermute | solution.py:410
where the time goes:
time: 82.3 us; the launch traced here: 82.1 us
  starting transfers between devices  47.4 us (58%)
  waiting for transfers between devices  21.1 us (26%)
  Pallas kernels  13.4 us (16%)
    ppermute x34, starting transfers between devices, swap(): lax.ppermute(value, axis, [(i, i ^ flip) for i in range(lax.axis_size(axi...  46.5 us
    ppermute x34, waiting for transfers between devices, swap(): lax.ppermute(value, axis, [(i, i ^ flip) for i in range(lax.axis_size(axi...  17.1 us
    pallas_call x20, Pallas kernels, place_and_run(): return run(*placed)  13.4 us
    ppermute x1, waiting for transfers between devices, on_device(): lax.ppermute(leaving, 'dom', [(i, (i + 1) % domains) for i in range(domai...  3.94 us
  transfers between devices with their start and end apart: 35, of which 11 were waited for; matrix products, arithmetic and copies ran while one was open for 0% of the time, Pallas kernels for 12%

commit v1 on v0

--- a/solution.py
+++ b/solution.py
@@ -19,6 +19,14 @@
 
 def swap(value, axis, flip):
     return lax.ppermute(value, axis, [(i, i ^ flip) for i in range(lax.axis_size(axis))])
+
+
+def far_order(domains, name):
+    half = domains // 2
+    others = [*range(domains - 2, half, -1)]
+    if name == "two":
+        others.reverse()
+    return [half, domains - 1, *others]
 
 
 def block(shape, dtype=BF16):
@@ -132,7 +140,7 @@
         outs[k - 1][0] = pair_ref[which_ref[k]]
 
 
-def fill_early_kernel(domains, own_ref, *refs):
+def fill_early_kernel(domains, name, own_ref, *refs):
     *arrived, pool_ref = refs
     half = domains // 2
     rows = own_ref.shape[0]
@@ -140,14 +148,13 @@
     pool_ref[rows : rows + 2] = arrived[0][...]
     for k in range(1, half):
         pool_ref[rows + 2 * k : rows + 2 * k + 2] = arrived[k][...]
-    pool_ref[rows + 2 * half + 1] = arrived[half][0]
-    for k in range(half + 2, domains):
-        pool_ref[rows + 2 * k + 1] = arrived[k - 1][0]
-
-
-def fill_late(domains, rows, late, pool_ref):
-    half = domains // 2
-    pool_ref[rows + 2 * (half + 1) + 1] = late[0][0]
+    for k, ref in zip(far_order(domains, name)[:-1], arrived[half:], strict=True):
+        pool_ref[rows + 2 * k + 1] = ref[0]
+
+
+def fill_late(domains, name, rows, late, pool_ref):
+    half = domains // 2
+    pool_ref[rows + 2 * far_order(domains, name)[-1] + 1] = late[0][0]
     for k in range(1, half):
         pool_ref[rows + 2 * (half + k)] = late[k][0]
 
@@ -168,7 +175,7 @@
 
 def first_sum_kernel(domains, feats, part, table_ref, deal_ref, adjacency_ref, *refs):
     _, *late, pool_ref, out_ref = refs
-    fill_late(domains, adjacency_ref.shape[0], late, pool_ref)
+    fill_late(domains, "one", adjacency_ref.shape[0], late, pool_ref)
     part_sum_kernel(feats, [part], table_ref, deal_ref, adjacency_ref, pool_ref, out_ref)
 
 
@@ -180,10 +187,9 @@
 
 def leaving_sum_kernel(domains, table_ref, slots_ref, adjacency_ref, *refs):
     _, *late, pool_ref, out_ref = refs
-    fill_late(domains, adjacency_ref.shape[0], late, pool_ref)
-
-    @pl.loop(0, out_ref.shape[0])
-    def _(i):
+    fill_late(domains, "two", adjacency_ref.shape[0], late, pool_ref)
+
+    for i in range(out_ref.shape[0]):
         out_ref[i] = sum_row(slots_ref[i], table_ref, adjacency_ref, pool_ref)
 
 
@@ -276,7 +282,7 @@
     return place_and_run
 
 
-def exchange(domains, own, pair, sends, which):
+def exchange(domains, own, pair, sends, which, name):
     half = domains // 2
     shape = pair.shape[1:]
     near, far = sends[: half - 1], sends[half - 1 :]
@@ -291,15 +297,16 @@
         moved=4 * pair.size * half,
     )(which, pair)
     relay = [swap(relay[k - 1], "dom", k) for k in range(1, half)]
-    early = [pair, *near, far[0], *far[2:]]
+    far = [far[k - half] for k in far_order(domains, name)]
+    early = [pair, *near, *far[:-1]]
     pool = call(
-        functools.partial(fill_early_kernel, domains),
+        functools.partial(fill_early_kernel, domains, name),
         [block((own.shape[0] + 2 * domains, *shape))],
         [VMEM] * (1 + len(early)),
         [VMEM],
         moved=8 * own.size,
     )(own, *early)[0]
-    return [pool, far[1], *relay]
+    return [pool, far[-1], *relay]
 
 
 def on_device(features, adjacency, tile_src, mig_slot, weight_one, weight_two):
@@ -335,7 +342,7 @@
         [SMEM] * 3 + [VMEM] * len(near_far),
         moved=8 * size * width * domains,
     )(mig, named, own)
-    arrived = exchange(domains, own, pair, sends, which)
+    arrived = exchange(domains, own, pair, sends, which, "one")
     loaded = (adjacency, weight_one, weight_two)
     table, adjacency, weight_one, weight_two = call(
         functools.partial(table_kernel, domains, rows),
@@ -396,7 +403,7 @@
         [VMEM] * (1 + len(near_far)),
         moved=8 * size * width * domains,
     )(slots, deal, *columns)
-    arrived = exchange(domains, own, pair, sends, which)
+    arrived = exchange(domains, own, pair, sends, which, "two")
 
     pool_two, leaving = call(
         functools.partial(leaving_sum_kernel, domains),

time: 82.3 us -> 81.3 us (0.988)
  starting transfers between devices: 47.4 us -> 46.3 us
    ppermute x34, starting transfers between devices: 46.5 us -> 44.9 us  [swap(): lax.ppermute(value, axis, [(i, i ^ flip) for i in range(lax.axis_size(axi...]
    ppermute x34, waiting for transfers between devices: 17.1 us -> 18 us  [swap(): lax.ppermute(value, axis, [(i, i ^ flip) for i in range(lax.axis_size(axi...]
where the time goes in v1:
time: 81.3 us; the launch traced here: 81.1 us
  starting transfers between devices  46.3 us (57%)
  waiting for transfers between devices  21.4 us (26%)
  Pallas kernels  13.2 us (16%)
    ppermute x34, starting transfers between devices, swap(): lax.ppermute(value, axis, [(i, i ^ flip) for i in range(lax.axis_size(axi...  44.9 us
    ppermute x34, waiting for transfers between devices, swap(): lax.ppermute(value, axis, [(i, i ^ flip) for i in range(lax.axis_size(axi...  18 us
    pallas_call x20, Pallas kernels, place_and_run(): return run(*placed)  13.2 us
    ppermute x1, waiting for transfers between devices, on_device(): lax.ppermute(leaving, 'dom', [(i, (i + 1) % domains) for i in range(domai...  3.45 us
  transfers between devices with their start and end apart: 35, of which 11 were waited for; matrix products, arithmetic and copies ran while one was open for 0% of the time, Pallas kernels for 12%

profile of v1, /device:TPU:0, one launch (start us, length us, event | category | flops | bytes accessed | tf_op | source)
XLA Modules:
  0.0 81.1 jit_solution(1457945225121193898)
XLA Ops:
  0.0 1.1 %shard_map.64 = (s32[16,64]{1,0:T(8,128)S(1)}, s32[2,8]{1,0:T(2,128)S(4)}, bf16[8,128,256]{2,1,0:T(8,128)(2,1)S(1)}, bf16[2,128,256]{2,1,0:T(8,128)(2,1)S(1)}) custom-call(s32[16,64]{1,0:T(8,128)} %bitcast.5, s32[2,8]{1,0:T(2,128)} %bitcast.6, bf16[8,128,256]{2,1,0:T(8,128)(2,1)} %bitcast.4), custom_call_target="tpu_custom_call" | custom-call | bytes 524288 | tf_op jit(solution)/shard_map/pallas_call | solution.py:280
  1.1 4.1 %collective-permute-start = (bf16[2,128,256]{2,1,0:T(8,128)(2,1)S(1)}, bf16[2,128,256]{2,1,0:T(8,128)(2,1)S(1)}, u32[]{:S(2)}, u32[]{:S(2)}) collective-permute-start(bf16[2,128,256]{2,1,0:T(8,128)(2,1)S(1)} %get-tuple-element.62), channel_id=1, source_target_pairs={{0,16},{4,20},{8,24},{12,28},{16,0},{20,4},{24,8},{28,12},{1,17},{... | collective-permute-start | bytes 393224 | tf_op jit(solution)/shard_map/ppermute | solution.py:21
  5.2 0.3 shard_map.65
  5.6 1.8 %collective-permute-start.1 = (bf16[2,128,256]{2,1,0:T(8,128)(2,1)S(1)}, bf16[2,128,256]{2,1,0:T(8,128)(2,1)S(1)}, u32[]{:S(2)}, u32[]{:S(2)}) collective-permute-start(bf16[2,128,256]{2,1,0:T(8,128)(2,1)S(1)} %get-tuple-element.63), channel_id=1, source_target_pairs={{0,4},{4,0},{8,12},{12,8},{16,20},{20,16},{24,28},{28,24},{1,5},{5... | collective-permute-start | bytes 393224 | tf_op jit(solution)/shard_map/ppermute | solution.py:21
  7.4 1.6 %collective-permute-start.2 = (bf16[2,128,256]{2,1,0:T(8,128)(2,1)S(1)}, bf16[2,128,256]{2,1,0:T(8,128)(2,1)S(1)}, u32[]{:S(2)}, u32[]{:S(2)}) collective-permute-start(bf16[2,128,256]{2,1,0:T(8,128)(2,1)S(1)} %get-tuple-element.64), channel_id=1, source_target_pairs={{0,8},{4,12},{8,0},{12,4},{16,24},{20,28},{24,16},{28,20},{1,9},{5... | collective-permute-start | bytes 393224 | tf_op jit(solution)/shard_map/ppermute | solution.py:21
  9.0 2.4 %collective-permute-start.5 = (bf16[1,128,256]{2,1,0:T(8,128)(2,1)S(1)}, bf16[1,128,256]{2,1,0:T(8,128)(2,1)S(1)}, u32[]{:S(2)}, u32[]{:S(2)}) collective-permute-start(bf16[1,128,256]{2,1,0:T(8,128)(2,1)S(1)} %get-tuple-element.67), channel_id=1, source_target_pairs={{0,28},{4,24},{8,20},{12,16},{16,12},{20,8},{24,4},{28,0},{1,29},{... | collective-permute-start | bytes 196616 | tf_op jit(solution)/shard_map/ppermute | solution.py:21
  11.4 5.0 %collective-permute-done.4.refs_4_ = bf16[1,128,256]{2,1,0:T(8,128)(2,1)S(1)} collective-permute-done((bf16[1,128,256]{2,1,0:T(8,128)(2,1)S(1)}, bf16[1,128,256]{2,1,0:T(8,128)(2,1)S(1)}, u32[]{:S(2)}, u32[]{:S(2)}) %collective-permute-start.4) | collective-permute-done | bytes 65568 | tf_op jit(solution)/shard_map/ppermute | solution.py:21
  16.5 3.0 %collective-permute-start.6 = (bf16[1,128,256]{2,1,0:T(8,128)(2,1)S(1)}, bf16[1,128,256]{2,1,0:T(8,128)(2,1)S(1)}, u32[]{:S(2)}, u32[]{:S(2)}) collective-permute-start(bf16[1,128,256]{2,1,0:T(8,128)(2,1)S(1)} %get-tuple-element.68), channel_id=1, source_target_pairs={{0,24},{4,28},{8,16},{12,20},{16,8},{20,12},{24,0},{28,4},{1,25},{... | collective-permute-start | bytes 196616 | tf_op jit(solution)/shard_map/ppermute | solution.py:21
  19.5 2.4 %collective-permute-start.7 = (bf16[1,128,256]{2,1,0:T(8,128)(2,1)S(1)}, bf16[1,128,256]{2,1,0:T(8,128)(2,1)S(1)}, u32[]{:S(2)}, u32[]{:S(2)}) collective-permute-start(bf16[1,128,256]{2,1,0:T(8,128)(2,1)S(1)} %get-tuple-element.69), channel_id=1, source_target_pairs={{0,20},{4,16},{8,28},{12,24},{16,4},{20,0},{24,12},{28,8},{1,21},{... | collective-permute-start | bytes 196616 | tf_op jit(solution)/shard_map/ppermute | solution.py:21
  21.8 1.3 %collective-permute-done.6.refs_6_ = bf16[1,128,256]{2,1,0:T(8,128)(2,1)S(1)} collective-permute-done((bf16[1,128,256]{2,1,0:T(8,128)(2,1)S(1)}, bf16[1,128,256]{2,1,0:T(8,128)(2,1)S(1)}, u32[]{:S(2)}, u32[]{:S(2)}) %collective-permute-start.6) | collective-permute-done | bytes 65568 | tf_op jit(solution)/shard_map/ppermute | solution.py:21
  23.1 1.6 %collective-permute-start.8 = (bf16[1,128,256]{2,1,0:T(8,128)(2,1)S(1)}, bf16[1,128,256]{2,1,0:T(8,128)(2,1)S(1)}, u32[]{:S(2)}, u32[]{:S(2)}) collective-permute-start(bf16[1,128,256]{2,1,0:T(8,128)(2,1)S(1)} %get-tuple-element.71), channel_id=1, source_target_pairs={{0,4},{4,0},{8,12},{12,8},{16,20},{20,16},{24,28},{28,24},{1,5},{5... | collective-permute-start | bytes 196616 | tf_op jit(solution)/shard_map/ppermute | solution.py:21
  24.7 1.9 %collective-permute-start.10 = (bf16[1,128,256]{2,1,0:T(8,128)(2,1)S(1)}, bf16[1,128,256]{2,1,0:T(8,128)(2,1)S(1)}, u32[]{:S(2)}, u32[]{:S(2)}) collective-permute-start(bf16[1,128,256]{2,1,0:T(8,128)(2,1)S(1)} %get-tuple-element.73), channel_id=1, source_target_pairs={{0,12},{4,8},{8,4},{12,0},{16,28},{20,24},{24,20},{28,16},{1,13},{... | collective-permute-start | bytes 196616 | tf_op jit(solution)/shard_map/ppermute | solution.py:21
  26.6 3.5 %shard_map.66 = (s32[16,64]{1,0:T(8,128)S(4)}, bf16[8,16,128,128]{3,2,1,0:T(8,128)(2,1)S(1)}, bf16[1024,1024]{1,0:T(8,128)(2,1)S(1)}, bf16[1024,1024]{1,0:T(8,128)(2,1)S(1)}) custom-call(s32[2,8]{1,0:T(2,128)S(4)} %get-tuple-element.53.mig, s32[16,64]{1,0:T(8,128)S(1)} %get-tuple-element.54.tiles_ref, bf16[8,16,128,128]{3,2,1,0:T(8,128)(2,1)} %refs_0_.1, ...), custom_call_target="tpu_custom_call" | custom-call | bytes 8388608 | tf_op jit(solution)/shard_map/pallas_call | solution.py:280
  30.3 0.3 shard_map.69
  30.6 0.5 shard_map.70
  31.2 0.3 shard_map.71
  31.6 1.6 %collective-permute-start.12 = (bf16[1,128,256]{2,1,0:T(8,128)(2,1)S(1)}, bf16[1,128,256]{2,1,0:T(8,128)(2,1)S(1)}, u32[]{:S(2)}, u32[]{:S(2)}) collective-permute-start(bf16[1,128,256]{2,1,0:T(8,128)(2,1)S(1)} %get-tuple-element.77), channel_id=1, source_target_pairs={{0,2},{1,3},{2,0},{3,1},{4,6},{5,7},{6,4},{7,5},{8,10},{9,11},{10,... | collective-permute-start | bytes 196616 | tf_op jit(solution)/shard_map/ppermute | solution.py:21
  33.4 0.5 shard_map.73
  33.9 0.4 collective-permute-start.17
  34.4 0.3 shard_map.74
  34.7 1.6 %collective-permute-start.18 = (bf16[1,128,256]{2,1,0:T(8,128)(2,1)S(1)}, bf16[1,128,256]{2,1,0:T(8,128)(2,1)S(1)}, u32[]{:S(2)}, u32[]{:S(2)}) collective-permute-start(bf16[1,128,256]{2,1,0:T(8,128)(2,1)S(1)} %shard_map.74), channel_id=1, source_target_pairs={{0,2},{1,3},{2,0},{3,1},{4,6},{5,7},{6,4},{7,5},{8,10},{9,11},{10,... | collective-permute-start | bytes 196616 | tf_op jit(solution)/shard_map/ppermute | solution.py:21
  36.3 0.3 shard_map.75
  36.7 0.5 collective-permute-done.13.refs_3_
  37.2 0.8 shard_map.72
  38.3 1.4 %collective-permute-start.15 = (bf16[1,128,256]{2,1,0:T(8,128)(2,1)S(1)}, bf16[1,128,256]{2,1,0:T(8,128)(2,1)S(1)}, u32[]{:S(2)}, u32[]{:S(2)}) collective-permute-start(bf16[1,128,256]{2,1,0:T(8,128)(2,1)S(1)} %get-tuple-element.80), channel_id=1, source_target_pairs={{0,2},{1,3},{2,0},{3,1},{4,6},{5,7},{6,4},{7,5},{8,10},{9,11},{10,... | collective-permute-start | bytes 196616 | tf_op jit(solution)/shard_map/ppermute | solution.py:21
  39.9 1.1 %collective-permute-done.19.refs_3_ = bf16[1,128,256]{2,1,0:T(8,128)(2,1)S(1)} collective-permute-done((bf16[1,128,256]{2,1,0:T(8,128)(2,1)S(1)}, bf16[1,128,256]{2,1,0:T(8,128)(2,1)S(1)}, u32[]{:S(2)}, u32[]{:S(2)}) %collective-permute-start.19) | collective-permute-done | bytes 65568 | tf_op jit(solution)/shard_map/ppermute | solution.py:21
  41.0 0.8 shard_map.76
  42.0 0.7 collective-permute-start.21
  42.7 1.0 %collective-permute-start.22 = (bf16[1,128,256]{2,1,0:T(8,128)(2,1)S(1)}, bf16[1,128,256]{2,1,0:T(8,128)(2,1)S(1)}, u32[]{:S(2)}, u32[]{:S(2)}) collective-permute-start(bf16[1,128,256]{2,1,0:T(8,128)(2,1)S(1)} %get-tuple-element.87), channel_id=1, source_target_pairs={{0,3},{1,2},{2,1},{3,0},{4,7},{5,6},{6,5},{7,4},{8,11},{9,10},{10,... | collective-permute-start | bytes 196616 | tf_op jit(solution)/shard_map/ppermute | solution.py:21
  43.7 0.3 collective-permute-done.16.refs_3_
  44.1 3.2 %collective-permute-start.23 = (bf16[2,128,256]{2,1,0:T(8,128)(2,1)S(1)}, bf16[2,128,256]{2,1,0:T(8,128)(2,1)S(1)}, u32[]{:S(2)}, u32[]{:S(2)}) collective-permute-start(bf16[2,128,256]{2,1,0:T(8,128)(2,1)S(1)} %shard_map.78), channel_id=1, source_target_pairs={{0,16},{4,20},{8,24},{12,28},{16,0},{20,4},{24,8},{28,12},{1,17},{... | collective-permute-start | bytes 393224 | tf_op jit(solution)/shard_map/ppermute | solution.py:21
  47.4 3.1 %collective-permute-start.27 = (bf16[1,128,256]{2,1,0:T(8,128)(2,1)S(1)}, bf16[1,128,256]{2,1,0:T(8,128)(2,1)S(1)}, u32[]{:S(2)}, u32[]{:S(2)}) collective-permute-start(bf16[1,128,256]{2,1,0:T(8,128)(2,1)S(1)} %get-tuple-element.92), channel_id=1, source_target_pairs={{0,16},{4,20},{8,24},{12,28},{16,0},{20,4},{24,8},{28,12},{1,17},{... | collective-permute-start | bytes 196616 | tf_op jit(solution)/shard_map/ppermute | solution.py:21
  50.6 0.5 collective-permute-start.24
  51.0 1.5 %collective-permute-start.25 = (bf16[2,128,256]{2,1,0:T(8,128)(2,1)S(1)}, bf16[2,128,256]{2,1,0:T(8,128)(2,1)S(1)}, u32[]{:S(2)}, u32[]{:S(2)}) collective-permute-start(bf16[2,128,256]{2,1,0:T(8,128)(2,1)S(1)} %get-tuple-element.90), channel_id=1, source_target_pairs={{0,8},{4,12},{8,0},{12,4},{16,24},{20,28},{24,16},{28,20},{1,9},{5... | collective-permute-start | bytes 393224 | tf_op jit(solution)/shard_map/ppermute | solution.py:21
  52.5 1.0 %collective-permute-start.28 = (bf16[1,128,256]{2,1,0:T(8,128)(2,1)S(1)}, bf16[1,128,256]{2,1,0:T(8,128)(2,1)S(1)}, u32[]{:S(2)}, u32[]{:S(2)}) collective-permute-start(bf16[1,128,256]{2,1,0:T(8,128)(2,1)S(1)} %get-tuple-element.93), channel_id=1, source_target_pairs={{0,28},{4,24},{8,20},{12,16},{16,12},{20,8},{24,4},{28,0},{1,29},{... | collective-permute-start | bytes 196616 | tf_op jit(solution)/shard_map/ppermute | solution.py:21
  53.6 5.2 %collective-permute-done.27.refs_4_ = bf16[1,128,256]{2,1,0:T(8,128)(2,1)S(1)} collective-permute-done((bf16[1,128,256]{2,1,0:T(8,128)(2,1)S(1)}, bf16[1,128,256]{2,1,0:T(8,128)(2,1)S(1)}, u32[]{:S(2)}, u32[]{:S(2)}) %collective-permute-start.27) | collective-permute-done | bytes 65568 | tf_op jit(solution)/shard_map/ppermute | solution.py:21
  58.7 4.8 %collective-permute-start.26 = (bf16[2,128,256]{2,1,0:T(8,128)(2,1)S(1)}, bf16[2,128,256]{2,1,0:T(8,128)(2,1)S(1)}, u32[]{:S(2)}, u32[]{:S(2)}) collective-permute-start(bf16[2,128,256]{2,1,0:T(8,128)(2,1)S(1)} %get-tuple-element.91), channel_id=1, source_target_pairs={{0,12},{4,8},{8,4},{12,0},{16,28},{20,24},{24,20},{28,16},{1,13},{... | collective-permute-start | bytes 393224 | tf_op jit(solution)/shard_map/ppermute | solution.py:21
  63.6 0.5 collective-permute-start.30
  64.1 1.5 %collective-permute-done.29.refs_6_ = bf16[1,128,256]{2,1,0:T(8,128)(2,1)S(1)} collective-permute-done((bf16[1,128,256]{2,1,0:T(8,128)(2,1)S(1)}, bf16[1,128,256]{2,1,0:T(8,128)(2,1)S(1)}, u32[]{:S(2)}, u32[]{:S(2)}) %collective-permute-start.29) | collective-permute-done | bytes 65568 | tf_op jit(solution)/shard_map/ppermute | solution.py:21
  65.6 1.4 %collective-permute-start.32 = (bf16[1,128,256]{2,1,0:T(8,128)(2,1)S(1)}, bf16[1,128,256]{2,1,0:T(8,128)(2,1)S(1)}, u32[]{:S(2)}, u32[]{:S(2)}) collective-permute-start(bf16[1,128,256]{2,1,0:T(8,128)(2,1)S(1)} %get-tuple-element.97), channel_id=1, source_target_pairs={{0,8},{4,12},{8,0},{12,4},{16,24},{20,28},{24,16},{28,20},{1,9},{5... | collective-permute-start | bytes 196616 | tf_op jit(solution)/shard_map/ppermute | solution.py:21
  67.0 2.1 %collective-permute-start.33 = (bf16[1,128,256]{2,1,0:T(8,128)(2,1)S(1)}, bf16[1,128,256]{2,1,0:T(8,128)(2,1)S(1)}, u32[]{:S(2)}, u32[]{:S(2)}) collective-permute-start(bf16[1,128,256]{2,1,0:T(8,128)(2,1)S(1)} %get-tuple-element.98), channel_id=1, source_target_pairs={{0,12},{4,8},{8,4},{12,0},{16,28},{20,24},{24,20},{28,16},{1,13},{... | collective-permute-start | bytes 196616 | tf_op jit(solution)/shard_map/ppermute | solution.py:21
  69.2 1.1 %collective-permute-done.30.refs_1_ = bf16[1,128,256]{2,1,0:T(8,128)(2,1)S(1)} collective-permute-done((bf16[1,128,256]{2,1,0:T(8,128)(2,1)S(1)}, bf16[1,128,256]{2,1,0:T(8,128)(2,1)S(1)}, u32[]{:S(2)}, u32[]{:S(2)}) %collective-permute-start.30) | collective-permute-done | bytes 65568 | tf_op jit(solution)/shard_map/ppermute | solution.py:21
  70.4 1.8 %collective-permute-done.33.refs_4_ = bf16[1,128,256]{2,1,0:T(8,128)(2,1)S(1)} collective-permute-done((bf16[1,128,256]{2,1,0:T(8,128)(2,1)S(1)}, bf16[1,128,256]{2,1,0:T(8,128)(2,1)S(1)}, u32[]{:S(2)}, u32[]{:S(2)}) %collective-permute-start.33) | collective-permute-done | bytes 65568 | tf_op jit(solution)/shard_map/ppermute | solution.py:21
  72.2 0.5 shard_map.81
  72.7 1.3 %collective-permute-start.34 = (bf16[2,128,256]{2,1,0:T(8,128)(2,1)S(1)}, bf16[2,128,256]{2,1,0:T(8,128)(2,1)S(1)}, u32[]{:S(2)}, u32[]{:S(2)}) collective-permute-start(bf16[2,128,256]{2,1,0:T(8,128)(2,1)S(1)} %get-tuple-element.99), channel_id=1, source_target_pairs={{0,4},{4,8},{8,12},{12,16},{16,20},{20,24},{24,28},{28,0},{1,5},{5... | collective-permute-start | bytes 393224 | tf_op jit(solution)/shard_map/ppermute | solution.py:417
  74.1 2.9 %shard_map.82.out_in_ref = bf16[8,128,256]{2,1,0:T(8,128)(2,1)} custom-call(s32[16,64]{1,0:T(8,128)S(4)} %get-tuple-element.57.table_ref, s32[16]{0:T(128)S(4)} %get-tuple-element.56.slots_ref, bf16[8,16,128,128]{3,2,1,0:T(8,128)(2,1)S(1)} %get-tuple-element.58.adjacency_ref, bf16[24,128,256]{2,1,0:T(8,128)(2,1)S(1)} %get-tuple-element.100.pool_ref), custom_call_target="tpu_custom_call" | custom-call | flops 805306368 | bytes 3145728 | tf_op jit(solution)/shard_map/pallas_call | solution.py:280
  77.0 3.5 %collective-permute-done.34.moved_ref = bf16[2,128,256]{2,1,0:T(8,128)(2,1)S(1)} collective-permute-done((bf16[2,128,256]{2,1,0:T(8,128)(2,1)S(1)}, bf16[2,128,256]{2,1,0:T(8,128)(2,1)S(1)}, u32[]{:S(2)}, u32[]{:S(2)}) %collective-permute-start.34) | collective-permute-done | bytes 131104 | tf_op jit(solution)/shard_map/ppermute | solution.py:417
  80.4 0.7 shard_map.83
  (42 shorter events, 1.8 us)
Async XLA Ops:
  1.1 18.3 %collective-permute-start = (bf16[2,128,256]{2,1,0:T(8,128)(2,1)S(1)}, bf16[2,128,256]{2,1,0:T(8,128)(2,1)S(1)}, u32[]{:S(2)}, u32[]{:S(2)}) collective-permute-start(bf16[2,128,256]{2,1,0:T(8,128)(2,1)S(1)} %get-tuple-element.62), channel_id=1, source_target_pairs={{0,16},{4,20},{8,24},{12,28},{16,0},{20,4},{24,8},{28,12},{1,17},{... | collective-permute-start | bytes 393224 | tf_op jit(solution)/shard_map/ppermute | solution.py:21
  5.5 10.9 %collective-permute-start.4 = (bf16[1,128,256]{2,1,0:T(8,128)(2,1)S(1)}, bf16[1,128,256]{2,1,0:T(8,128)(2,1)S(1)}, u32[]{:S(2)}, u32[]{:S(2)}) collective-permute-start(bf16[1,128,256]{2,1,0:T(8,128)(2,1)S(1)} %get-tuple-element.66), channel_id=1, source_target_pairs={{0,16},{4,20},{8,24},{12,28},{16,0},{20,4},{24,8},{28,12},{1,17},{... | collective-permute-start | bytes 196616 | tf_op jit(solution)/shard_map/ppermute | solution.py:21
  5.6 19.1 %collective-permute-start.1 = (bf16[2,128,256]{2,1,0:T(8,128)(2,1)S(1)}, bf16[2,128,256]{2,1,0:T(8,128)(2,1)S(1)}, u32[]{:S(2)}, u32[]{:S(2)}) collective-permute-start(bf16[2,128,256]{2,1,0:T(8,128)(2,1)S(1)} %get-tuple-element.63), channel_id=1, source_target_pairs={{0,4},{4,0},{8,12},{12,8},{16,20},{20,16},{24,28},{28,24},{1,5},{5... | collective-permute-start | bytes 393224 | tf_op jit(solution)/shard_map/ppermute | solution.py:21
  7.4 17.3 %collective-permute-start.2 = (bf16[2,128,256]{2,1,0:T(8,128)(2,1)S(1)}, bf16[2,128,256]{2,1,0:T(8,128)(2,1)S(1)}, u32[]{:S(2)}, u32[]{:S(2)}) collective-permute-start(bf16[2,128,256]{2,1,0:T(8,128)(2,1)S(1)} %get-tuple-element.64), channel_id=1, source_target_pairs={{0,8},{4,12},{8,0},{12,4},{16,24},{20,28},{24,16},{28,20},{1,9},{5... | collective-permute-start | bytes 393224 | tf_op jit(solution)/shard_map/ppermute | solution.py:21
  9.0 10.5 %collective-permute-start.5 = (bf16[1,128,256]{2,1,0:T(8,128)(2,1)S(1)}, bf16[1,128,256]{2,1,0:T(8,128)(2,1)S(1)}, u32[]{:S(2)}, u32[]{:S(2)}) collective-permute-start(bf16[1,128,256]{2,1,0:T(8,128)(2,1)S(1)} %get-tuple-element.67), channel_id=1, source_target_pairs={{0,28},{4,24},{8,20},{12,16},{16,12},{20,8},{24,4},{28,0},{1,29},{... | collective-permute-start | bytes 196616 | tf_op jit(solution)/shard_map/ppermute | solution.py:21
  16.5 6.7 %collective-permute-start.6 = (bf16[1,128,256]{2,1,0:T(8,128)(2,1)S(1)}, bf16[1,128,256]{2,1,0:T(8,128)(2,1)S(1)}, u32[]{:S(2)}, u32[]{:S(2)}) collective-permute-start(bf16[1,128,256]{2,1,0:T(8,128)(2,1)S(1)} %get-tuple-element.68), channel_id=1, source_target_pairs={{0,24},{4,28},{8,16},{12,20},{16,8},{20,12},{24,0},{28,4},{1,25},{... | collective-permute-start | bytes 196616 | tf_op jit(solution)/shard_map/ppermute | solution.py:21
  19.4 10.7 %collective-permute-start.3 = (bf16[2,128,256]{2,1,0:T(8,128)(2,1)S(1)}, bf16[2,128,256]{2,1,0:T(8,128)(2,1)S(1)}, u32[]{:S(2)}, u32[]{:S(2)}) collective-permute-start(bf16[2,128,256]{2,1,0:T(8,128)(2,1)S(1)} %get-tuple-element.65), channel_id=1, source_target_pairs={{0,12},{4,8},{8,4},{12,0},{16,28},{20,24},{24,20},{28,16},{1,13},{... | collective-permute-start | bytes 393224 | tf_op jit(solution)/shard_map/ppermute | solution.py:21
  19.5 10.8 %collective-permute-start.7 = (bf16[1,128,256]{2,1,0:T(8,128)(2,1)S(1)}, bf16[1,128,256]{2,1,0:T(8,128)(2,1)S(1)}, u32[]{:S(2)}, u32[]{:S(2)}) collective-permute-start(bf16[1,128,256]{2,1,0:T(8,128)(2,1)S(1)} %get-tuple-element.69), channel_id=1, source_target_pairs={{0,20},{4,16},{8,28},{12,24},{16,4},{20,0},{24,12},{28,8},{1,21},{... | collective-permute-start | bytes 196616 | tf_op jit(solution)/shard_map/ppermute | solution.py:21
  23.1 7.1 %collective-permute-start.8 = (bf16[1,128,256]{2,1,0:T(8,128)(2,1)S(1)}, bf16[1,128,256]{2,1,0:T(8,128)(2,1)S(1)}, u32[]{:S(2)}, u32[]{:S(2)}) collective-permute-start(bf16[1,128,256]{2,1,0:T(8,128)(2,1)S(1)} %get-tuple-element.71), channel_id=1, source_target_pairs={{0,4},{4,0},{8,12},{12,8},{16,20},{20,16},{24,28},{28,24},{1,5},{5... | collective-permute-start | bytes 196616 | tf_op jit(solution)/shard_map/ppermute | solution.py:21
  24.7 5.5 %collective-permute-start.9 = (bf16[1,128,256]{2,1,0:T(8,128)(2,1)S(1)}, bf16[1,128,256]{2,1,0:T(8,128)(2,1)S(1)}, u32[]{:S(2)}, u32[]{:S(2)}) collective-permute-start(bf16[1,128,256]{2,1,0:T(8,128)(2,1)S(1)} %get-tuple-element.72), channel_id=1, source_target_pairs={{0,8},{4,12},{8,0},{12,4},{16,24},{20,28},{24,16},{28,20},{1,9},{5... | collective-permute-start | bytes 196616 | tf_op jit(solution)/shard_map/ppermute | solution.py:21
  24.7 5.6 %collective-permute-start.10 = (bf16[1,128,256]{2,1,0:T(8,128)(2,1)S(1)}, bf16[1,128,256]{2,1,0:T(8,128)(2,1)S(1)}, u32[]{:S(2)}, u32[]{:S(2)}) collective-permute-start(bf16[1,128,256]{2,1,0:T(8,128)(2,1)S(1)} %get-tuple-element.73), channel_id=1, source_target_pairs={{0,12},{4,8},{8,4},{12,0},{16,28},{20,24},{24,20},{28,16},{1,13},{... | collective-permute-start | bytes 196616 | tf_op jit(solution)/shard_map/ppermute | solution.py:21
  31.5 5.1 %collective-permute-start.11 = (bf16[1,128,256]{2,1,0:T(8,128)(2,1)S(1)}, bf16[1,128,256]{2,1,0:T(8,128)(2,1)S(1)}, u32[]{:S(2)}, u32[]{:S(2)}) collective-permute-start(bf16[1,128,256]{2,1,0:T(8,128)(2,1)S(1)} %get-tuple-element.76), channel_id=1, source_target_pairs={{0,1},{1,0},{2,3},{3,2},{4,5},{5,4},{6,7},{7,6},{8,9},{9,8},{10,11... | collective-permute-start | bytes 196616 | tf_op jit(solution)/shard_map/ppermute | solution.py:21
  31.6 5.1 %collective-permute-start.12 = (bf16[1,128,256]{2,1,0:T(8,128)(2,1)S(1)}, bf16[1,128,256]{2,1,0:T(8,128)(2,1)S(1)}, u32[]{:S(2)}, u32[]{:S(2)}) collective-permute-start(bf16[1,128,256]{2,1,0:T(8,128)(2,1)S(1)} %get-tuple-element.77), channel_id=1, source_target_pairs={{0,2},{1,3},{2,0},{3,1},{4,6},{5,7},{6,4},{7,5},{8,10},{9,11},{10,... | collective-permute-start | bytes 196616 | tf_op jit(solution)/shard_map/ppermute | solution.py:21
  33.2 4.1 %collective-permute-start.13 = (bf16[1,128,256]{2,1,0:T(8,128)(2,1)S(1)}, bf16[1,128,256]{2,1,0:T(8,128)(2,1)S(1)}, u32[]{:S(2)}, u32[]{:S(2)}) collective-permute-start(bf16[1,128,256]{2,1,0:T(8,128)(2,1)S(1)} %shard_map.71), channel_id=1, source_target_pairs={{0,3},{1,2},{2,1},{3,0},{4,7},{5,6},{6,5},{7,4},{8,11},{9,10},{10,... | collective-permute-start | bytes 196616 | tf_op jit(solution)/shard_map/ppermute | solution.py:21
  33.9 5.8 %collective-permute-start.17 = (bf16[1,128,256]{2,1,0:T(8,128)(2,1)S(1)}, bf16[1,128,256]{2,1,0:T(8,128)(2,1)S(1)}, u32[]{:S(2)}, u32[]{:S(2)}) collective-permute-start(bf16[1,128,256]{2,1,0:T(8,128)(2,1)S(1)} %get-tuple-element.83), channel_id=1, source_target_pairs={{0,1},{1,0},{2,3},{3,2},{4,5},{5,4},{6,7},{7,6},{8,9},{9,8},{10,11... | collective-permute-start | bytes 196616 | tf_op jit(solution)/shard_map/ppermute | solution.py:21
  34.7 5.3 %collective-permute-start.18 = (bf16[1,128,256]{2,1,0:T(8,128)(2,1)S(1)}, bf16[1,128,256]{2,1,0:T(8,128)(2,1)S(1)}, u32[]{:S(2)}, u32[]{:S(2)}) collective-permute-start(bf16[1,128,256]{2,1,0:T(8,128)(2,1)S(1)} %shard_map.74), channel_id=1, source_target_pairs={{0,2},{1,3},{2,0},{3,1},{4,6},{5,7},{6,4},{7,5},{8,10},{9,11},{10,... | collective-permute-start | bytes 196616 | tf_op jit(solution)/shard_map/ppermute | solution.py:21
  36.6 4.4 %collective-permute-start.19 = (bf16[1,128,256]{2,1,0:T(8,128)(2,1)S(1)}, bf16[1,128,256]{2,1,0:T(8,128)(2,1)S(1)}, u32[]{:S(2)}, u32[]{:S(2)}) collective-permute-start(bf16[1,128,256]{2,1,0:T(8,128)(2,1)S(1)} %shard_map.75), channel_id=1, source_target_pairs={{0,3},{1,2},{2,1},{3,0},{4,7},{5,6},{6,5},{7,4},{8,11},{9,10},{10,... | collective-permute-start | bytes 196616 | tf_op jit(solution)/shard_map/ppermute | solution.py:21
  38.0 4.7 %collective-permute-start.14 = (bf16[1,128,256]{2,1,0:T(8,128)(2,1)S(1)}, bf16[1,128,256]{2,1,0:T(8,128)(2,1)S(1)}, u32[]{:S(2)}, u32[]{:S(2)}) collective-permute-start(bf16[1,128,256]{2,1,0:T(8,128)(2,1)S(1)} %get-tuple-element.79), channel_id=1, source_target_pairs={{0,1},{1,0},{2,3},{3,2},{4,5},{5,4},{6,7},{7,6},{8,9},{9,8},{10,11... | collective-permute-start | bytes 196616 | tf_op jit(solution)/shard_map/ppermute | solution.py:21
  38.3 5.4 %collective-permute-start.15 = (bf16[1,128,256]{2,1,0:T(8,128)(2,1)S(1)}, bf16[1,128,256]{2,1,0:T(8,128)(2,1)S(1)}, u32[]{:S(2)}, u32[]{:S(2)}) collective-permute-start(bf16[1,128,256]{2,1,0:T(8,128)(2,1)S(1)} %get-tuple-element.80), channel_id=1, source_target_pairs={{0,2},{1,3},{2,0},{3,1},{4,6},{5,7},{6,4},{7,5},{8,10},{9,11},{10,... | collective-permute-start | bytes 196616 | tf_op jit(solution)/shard_map/ppermute | solution.py:21
  39.7 4.4 %collective-permute-start.16 = (bf16[1,128,256]{2,1,0:T(8,128)(2,1)S(1)}, bf16[1,128,256]{2,1,0:T(8,128)(2,1)S(1)}, u32[]{:S(2)}, u32[]{:S(2)}) collective-permute-start(bf16[1,128,256]{2,1,0:T(8,128)(2,1)S(1)} %get-tuple-element.81), channel_id=1, source_target_pairs={{0,3},{1,2},{2,1},{3,0},{4,7},{5,6},{6,5},{7,4},{8,11},{9,10},{10,... | collective-permute-start | bytes 196616 | tf_op jit(solution)/shard_map/ppermute | solution.py:21
  41.8 5.5 %collective-permute-start.20 = (bf16[1,128,256]{2,1,0:T(8,128)(2,1)S(1)}, bf16[1,128,256]{2,1,0:T(8,128)(2,1)S(1)}, u32[]{:S(2)}, u32[]{:S(2)}) collective-permute-start(bf16[1,128,256]{2,1,0:T(8,128)(2,1)S(1)} %get-tuple-element.85), channel_id=1, source_target_pairs={{0,1},{1,0},{2,3},{3,2},{4,5},{5,4},{6,7},{7,6},{8,9},{9,8},{10,11... | collective-permute-start | bytes 196616 | tf_op jit(solution)/shard_map/ppermute | solution.py:21
  42.0 5.3 %collective-permute-start.21 = (bf16[1,128,256]{2,1,0:T(8,128)(2,1)S(1)}, bf16[1,128,256]{2,1,0:T(8,128)(2,1)S(1)}, u32[]{:S(2)}, u32[]{:S(2)}) collective-permute-start(bf16[1,128,256]{2,1,0:T(8,128)(2,1)S(1)} %get-tuple-element.86), channel_id=1, source_target_pairs={{0,2},{1,3},{2,0},{3,1},{4,6},{5,7},{6,4},{7,5},{8,10},{9,11},{10,... | collective-permute-start | bytes 196616 | tf_op jit(solution)/shard_map/ppermute | solution.py:21
  42.7 4.6 %collective-permute-start.22 = (bf16[1,128,256]{2,1,0:T(8,128)(2,1)S(1)}, bf16[1,128,256]{2,1,0:T(8,128)(2,1)S(1)}, u32[]{:S(2)}, u32[]{:S(2)}) collective-permute-start(bf16[1,128,256]{2,1,0:T(8,128)(2,1)S(1)} %get-tuple-element.87), channel_id=1, source_target_pairs={{0,3},{1,2},{2,1},{3,0},{4,7},{5,6},{6,5},{7,4},{8,11},{9,10},{10,... | collective-permute-start | bytes 196616 | tf_op jit(solution)/shard_map/ppermute | solution.py:21
  44.1 14.7 %collective-permute-start.23 = (bf16[2,128,256]{2,1,0:T(8,128)(2,1)S(1)}, bf16[2,128,256]{2,1,0:T(8,128)(2,1)S(1)}, u32[]{:S(2)}, u32[]{:S(2)}) collective-permute-start(bf16[2,128,256]{2,1,0:T(8,128)(2,1)S(1)} %shard_map.78), channel_id=1, source_target_pairs={{0,16},{4,20},{8,24},{12,28},{16,0},{20,4},{24,8},{28,12},{1,17},{... | collective-permute-start | bytes 393224 | tf_op jit(solution)/shard_map/ppermute | solution.py:21
  47.4 11.3 %collective-permute-start.27 = (bf16[1,128,256]{2,1,0:T(8,128)(2,1)S(1)}, bf16[1,128,256]{2,1,0:T(8,128)(2,1)S(1)}, u32[]{:S(2)}, u32[]{:S(2)}) collective-permute-start(bf16[1,128,256]{2,1,0:T(8,128)(2,1)S(1)} %get-tuple-element.92), channel_id=1, source_target_pairs={{0,16},{4,20},{8,24},{12,28},{16,0},{20,4},{24,8},{28,12},{1,17},{... | collective-permute-start | bytes 196616 | tf_op jit(solution)/shard_map/ppermute | solution.py:21
  50.6 15.0 %collective-permute-start.24 = (bf16[2,128,256]{2,1,0:T(8,128)(2,1)S(1)}, bf16[2,128,256]{2,1,0:T(8,128)(2,1)S(1)}, u32[]{:S(2)}, u32[]{:S(2)}) collective-permute-start(bf16[2,128,256]{2,1,0:T(8,128)(2,1)S(1)} %get-tuple-element.89), channel_id=1, source_target_pairs={{0,4},{4,0},{8,12},{12,8},{16,20},{20,16},{24,28},{28,24},{1,5},{5... | collective-permute-start | bytes 393224 | tf_op jit(solution)/shard_map/ppermute | solution.py:21
  51.0 16.0 %collective-permute-start.25 = (bf16[2,128,256]{2,1,0:T(8,128)(2,1)S(1)}, bf16[2,128,256]{2,1,0:T(8,128)(2,1)S(1)}, u32[]{:S(2)}, u32[]{:S(2)}) collective-permute-start(bf16[2,128,256]{2,1,0:T(8,128)(2,1)S(1)} %get-tuple-element.90), channel_id=1, source_target_pairs={{0,8},{4,12},{8,0},{12,4},{16,24},{20,28},{24,16},{28,20},{1,9},{5... | collective-permute-start | bytes 393224 | tf_op jit(solution)/shard_map/ppermute | solution.py:21
  52.5 11.0 %collective-permute-start.28 = (bf16[1,128,256]{2,1,0:T(8,128)(2,1)S(1)}, bf16[1,128,256]{2,1,0:T(8,128)(2,1)S(1)}, u32[]{:S(2)}, u32[]{:S(2)}) collective-permute-start(bf16[1,128,256]{2,1,0:T(8,128)(2,1)S(1)} %get-tuple-element.93), channel_id=1, source_target_pairs={{0,28},{4,24},{8,20},{12,16},{16,12},{20,8},{24,4},{28,0},{1,29},{... | collective-permute-start | bytes 196616 | tf_op jit(solution)/shard_map/ppermute | solution.py:21
  58.7 6.9 %collective-permute-start.29 = (bf16[1,128,256]{2,1,0:T(8,128)(2,1)S(1)}, bf16[1,128,256]{2,1,0:T(8,128)(2,1)S(1)}, u32[]{:S(2)}, u32[]{:S(2)}) collective-permute-start(bf16[1,128,256]{2,1,0:T(8,128)(2,1)S(1)} %get-tuple-element.94), channel_id=1, source_target_pairs={{0,20},{4,16},{8,28},{12,24},{16,4},{20,0},{24,12},{28,8},{1,21},{... | collective-permute-start | bytes 196616 | tf_op jit(solution)/shard_map/ppermute | solution.py:21
  58.7 10.4 %collective-permute-start.26 = (bf16[2,128,256]{2,1,0:T(8,128)(2,1)S(1)}, bf16[2,128,256]{2,1,0:T(8,128)(2,1)S(1)}, u32[]{:S(2)}, u32[]{:S(2)}) collective-permute-start(bf16[2,128,256]{2,1,0:T(8,128)(2,1)S(1)} %get-tuple-element.91), channel_id=1, source_target_pairs={{0,12},{4,8},{8,4},{12,0},{16,28},{20,24},{24,20},{28,16},{1,13},{... | collective-permute-start | bytes 393224 | tf_op jit(solution)/shard_map/ppermute | solution.py:21
  63.6 6.7 %collective-permute-start.30 = (bf16[1,128,256]{2,1,0:T(8,128)(2,1)S(1)}, bf16[1,128,256]{2,1,0:T(8,128)(2,1)S(1)}, u32[]{:S(2)}, u32[]{:S(2)}) collective-permute-start(bf16[1,128,256]{2,1,0:T(8,128)(2,1)S(1)} %get-tuple-element.95), channel_id=1, source_target_pairs={{0,24},{4,28},{8,16},{12,20},{16,8},{20,12},{24,0},{28,4},{1,25},{... | collective-permute-start | bytes 196616 | tf_op jit(solution)/shard_map/ppermute | solution.py:21
  65.6 4.7 %collective-permute-start.31 = (bf16[1,128,256]{2,1,0:T(8,128)(2,1)S(1)}, bf16[1,128,256]{2,1,0:T(8,128)(2,1)S(1)}, u32[]{:S(2)}, u32[]{:S(2)}) collective-permute-start(bf16[1,128,256]{2,1,0:T(8,128)(2,1)S(1)} %get-tuple-element.96), channel_id=1, source_target_pairs={{0,4},{4,0},{8,12},{12,8},{16,20},{20,16},{24,28},{28,24},{1,5},{5... | collective-permute-start | bytes 196616 | tf_op jit(solution)/shard_map/ppermute | solution.py:21
  65.6 4.8 %collective-permute-start.32 = (bf16[1,128,256]{2,1,0:T(8,128)(2,1)S(1)}, bf16[1,128,256]{2,1,0:T(8,128)(2,1)S(1)}, u32[]{:S(2)}, u32[]{:S(2)}) collective-permute-start(bf16[1,128,256]{2,1,0:T(8,128)(2,1)S(1)} %get-tuple-element.97), channel_id=1, source_target_pairs={{0,8},{4,12},{8,0},{12,4},{16,24},{20,28},{24,16},{28,20},{1,9},{5... | collective-permute-start | bytes 196616 | tf_op jit(solution)/shard_map/ppermute | solution.py:21
  67.0 5.2 %collective-permute-start.33 = (bf16[1,128,256]{2,1,0:T(8,128)(2,1)S(1)}, bf16[1,128,256]{2,1,0:T(8,128)(2,1)S(1)}, u32[]{:S(2)}, u32[]{:S(2)}) collective-permute-start(bf16[1,128,256]{2,1,0:T(8,128)(2,1)S(1)} %get-tuple-element.98), channel_id=1, source_target_pairs={{0,12},{4,8},{8,4},{12,0},{16,28},{20,24},{24,20},{28,16},{1,13},{... | collective-permute-start | bytes 196616 | tf_op jit(solution)/shard_map/ppermute | solution.py:21
  72.7 7.7 %collective-permute-start.34 = (bf16[2,128,256]{2,1,0:T(8,128)(2,1)S(1)}, bf16[2,128,256]{2,1,0:T(8,128)(2,1)S(1)}, u32[]{:S(2)}, u32[]{:S(2)}) collective-permute-start(bf16[2,128,256]{2,1,0:T(8,128)(2,1)S(1)} %get-tuple-element.99), channel_id=1, source_target_pairs={{0,4},{4,8},{8,12},{12,16},{16,20},{20,24},{24,28},{28,0},{1,5},{5... | collective-permute-start | bytes 393224 | tf_op jit(solution)/shard_map/ppermute | solution.py:417
